TPU v7x, 512 devices: a whole 4x4x16 slice. The times are simulated.
512 devices in a mesh: gx: 16 (over x_lo, y, core), gy: 32 (over z, x_hi).
Axes of the slice: x: 4 (x_hi: 2, x_lo: 2; x = x_hi * 2 + x_lo), y: 4, z: 16, core: 2. Of those that a mesh axis runs over, the one named last changes fastest.
Arguments:
- phase: float32 [128, 256, 256], P('gx', 'gy'), may hold values from -1 to 1
- solute: float32 [128, 256, 256], P('gx', 'gy'), may hold values from 0 to 1
- undercool: float32 [128, 256, 256], P('gx', 'gy'), may hold values from -1 to 1
- lift_weight: float32 [32, 2], replicated, may hold values from -4 to 4
- spectral_weight: float32 [2, 32, 32, 32, 1024], P(None, 'gx', 'gy'), may hold values from -6 to 6
- local_weight: float32 [32, 32], replicated, may hold values from -1 to 1
- local_bias: float32 [32], replicated, may hold values from -4 to 4
- proj_weight: float32 [32], replicated, may hold values from -1 to 1
- cotangent: float32 [128, 256, 256], P('gx', 'gy'), may hold values from -6 to 6
Outputs:
- phase_next: float32 [128, 256, 256], P('gx', 'gy')
- solute_next: float32 [128, 256, 256], P('gx', 'gy')
- predicted: float32 [128, 256, 256], P('gx', 'gy')
- grad_spectral: float32 [2, 32, 32, 32, 1024], P(None, 'gx', 'gy')
- grad_local: float32 [32, 32], replicated
- grad_proj: float32 [32], replicated
All inputs are finite; a program needn't handle non-finite values.
Results may differ from a plain program's by a relative error of at most 0.00029.
Values sent between devices are 32-bit elements; how exact they have to be, the bound alone decides.
A program may use at most 64 MiB of HBM per device.

v0:
```python
from functools import reduce
import math

import jax
import jax.numpy as jnp
from jax import lax
from jax.sharding import PartitionSpec as P

WIDTH = 32
KX = 32
KY = 32
KZ = 32


TIME_STEP = 0.05
COUPLING = 2.0
SOLID_DIFF = 0.05
LIQUID_DIFF = 1.0
PARTITION = 0.15
TRAP_RATE = 4.0
SOLUTE_MEAN = 0.5


def extended(cells, sides, width):
    for axis, dim in sides:
        count = lax.axis_size(axis)
        head = lax.slice_in_dim(cells, 0, width, axis=dim)
        tail = lax.slice_in_dim(cells, cells.shape[dim] - width, cells.shape[dim], axis=dim)
        cells = jnp.concatenate(
            [
                lax.ppermute(tail, axis, [(i, (i + 1) % count) for i in range(count)]),
                cells,
                lax.ppermute(head, axis, [((i + 1) % count, i) for i in range(count)]),
            ],
            axis=dim,
        )
    return cells


def diffusivity(phase_now):
    return SOLID_DIFF + (LIQUID_DIFF - SOLID_DIFF) * 0.5 * (1.0 - jnp.tanh(phase_now))


def update(phase_now, solute_now, undercool, phase_nb, solute_nb, diff_now, diff_nb):
    lap = reduce(jnp.add, phase_nb) - 6.0 * phase_now
    squares = 1.0 - phase_now * phase_now
    rate = (
        lap
        + phase_now
        - phase_now * phase_now * phase_now
        + COUPLING * squares * squares * (undercool - solute_now)
    )
    fluxes = [
        0.5 * (diff_now + diff_nb[index]) * (solute_nb[index] - solute_now) for index in range(6)
    ]
    divergence = reduce(jnp.add, fluxes)
    speed = TRAP_RATE * jnp.abs(rate)
    keff = (PARTITION + speed) / (1.0 + speed)
    phase_new = phase_now + TIME_STEP * rate
    solute_new = solute_now + TIME_STEP * (divergence + 0.5 * (1.0 - keff) * solute_now * rate)
    return (phase_new, solute_new)


def beside(padded):
    centre = padded[1:-1, 1:-1]
    return [
        padded[2:, 1:-1],
        padded[:-2, 1:-1],
        padded[1:-1, 2:],
        padded[1:-1, :-2],
        jnp.roll(centre, -1, 2),
        jnp.roll(centre, 1, 2),
    ]


def phase_sweep(phase_now, solute_now, undercool):
    padded = extended(jnp.stack([phase_now, solute_now]), (("gx", 1), ("gy", 2)), 1)
    phase_pad = padded[0]
    solute_pad = padded[1]
    diff_pad = diffusivity(phase_pad)
    return update(
        phase_now,
        solute_now,
        undercool,
        beside(phase_pad),
        beside(solute_pad),
        diff_pad[1:-1, 1:-1],
        beside(diff_pad),
    )


def signed_freq(indices, total):
    return jnp.where(indices < total // 2, indices, indices - total)


def wave_tables(freqs, positions, length, factor):
    product = freqs[:, None] * positions[None, :] % length
    angles = product.astype(jnp.float32) * (2.0 * math.pi / length)
    return (jnp.cos(angles) * factor, jnp.sin(angles) * factor)


def complex_mix(cosines, sines, data, pattern, orient):

    def apply(table, values):
        return jnp.einsum(pattern, table, values, precision=lax.Precision.HIGHEST)

    cos_real = apply(cosines, data[0])
    cos_imag = apply(cosines, data[1])
    sin_real = apply(sines, data[0])
    sin_imag = apply(sines, data[1])
    return jnp.stack([cos_real - orient * sin_imag, cos_imag + orient * sin_real])


def x_forward(data, factor):
    portion = lax.all_to_all(data, "gx", split_axis=1, concat_axis=2, tiled=True)
    length = portion.shape[2]
    cosines, sines = wave_tables(
        signed_freq(jnp.arange(KX, dtype=jnp.int32), KX),
        jnp.arange(length, dtype=jnp.int32),
        length,
        factor,
    )
    lines = complex_mix(cosines, sines, portion, "kx,wxyz->wkyz", -1.0)
    return lax.all_to_all(lines, "gx", split_axis=2, concat_axis=1, tiled=True)


def y_forward(data, factor):
    portion = lax.all_to_all(data, "gy", split_axis=1, concat_axis=3, tiled=True)
    length = portion.shape[3]
    cosines, sines = wave_tables(
        signed_freq(jnp.arange(KY, dtype=jnp.int32), KY),
        jnp.arange(length, dtype=jnp.int32),
        length,
        factor,
    )
    lines = complex_mix(cosines, sines, portion, "ky,wayz->wakz", -1.0)
    return lax.all_to_all(lines, "gy", split_axis=3, concat_axis=1, tiled=True)


def contract(weights, values):
    return jnp.einsum("abzoi,iabz->oabz", weights, values, precision=lax.Precision.HIGHEST)


def outer(left, right):
    return jnp.einsum("oabz,iabz->abzoi", left, right, precision=lax.Precision.HIGHEST)


def per_device(
    phase,
    solute,
    undercool,
    lift_weight,
    spectral_weight,
    local_weight,
    local_bias,
    proj_weight,
    cotangent,
):
    phase_mid, solute_mid = phase_sweep(phase, solute, undercool)
    phase_next, solute_next = phase_sweep(phase_mid, solute_mid, undercool)
    cells_x, cells_y, depth = phase.shape
    total_x = cells_x * lax.axis_size("gx")
    total_y = cells_y * lax.axis_size("gy")
    fields = jnp.stack([phase_next, solute_next - SOLUTE_MEAN])
    modes_z = jnp.arange(KZ, dtype=jnp.int32)
    zpos = jnp.arange(depth, dtype=jnp.int32)
    unit_z = jnp.ones((KZ,), jnp.float32)
    weights_z = jnp.where(modes_z == 0, 1.0, 2.0).astype(jnp.float32) / depth

    def z_forward(field, zfactor):
        cosines, sines = wave_tables(modes_z, zpos, depth, zfactor[:, None])
        tables = jnp.stack([cosines, -sines])
        return jnp.einsum("wxyz,rkz->rwxyk", field, tables, precision=lax.Precision.HIGHEST)

    def spectral_forward(field, zfactor, xfactor, yfactor):
        return y_forward(x_forward(z_forward(field, zfactor), xfactor), yfactor)

    lifted = jnp.einsum("wc,cxyz->wxyz", lift_weight, fields, precision=lax.Precision.HIGHEST)
    spectrum = spectral_forward(lifted, unit_z, 1.0, 1.0)
    own_x = spectrum.shape[2]
    own_y = spectrum.shape[3]
    shaped = spectral_weight.reshape(2, own_x, own_y, KZ, WIDTH, WIDTH)
    out_real = contract(shaped[0], spectrum[0]) - contract(shaped[1], spectrum[1])
    out_imag = contract(shaped[0], spectrum[1]) + contract(shaped[1], spectrum[0])
    spectral_out = jnp.stack([out_real, out_imag])
    ypos = lax.axis_index("gy") * cells_y + jnp.arange(cells_y, dtype=jnp.int32)
    portion = lax.all_gather(spectral_out, "gy", axis=3, tiled=True)
    freqs = signed_freq(jnp.arange(portion.shape[3], dtype=jnp.int32), KY)
    cosines, sines = wave_tables(ypos, freqs, total_y, 1.0 / total_y)
    back_y = complex_mix(cosines, sines, portion, "yk,wakz->wayz", 1.0)
    xpos = lax.axis_index("gx") * cells_x + jnp.arange(cells_x, dtype=jnp.int32)
    portion = lax.all_gather(back_y, "gx", axis=2, tiled=True)
    freqs = signed_freq(jnp.arange(portion.shape[2], dtype=jnp.int32), KX)
    cosines, sines = wave_tables(xpos, freqs, total_x, 1.0 / total_x)
    back_x = complex_mix(cosines, sines, portion, "xk,wkyz->wxyz", 1.0)
    cos_back, sin_back = wave_tables(modes_z, zpos, depth, weights_z[:, None])
    back_tables = jnp.stack([cos_back, -sin_back])
    spectral_field = jnp.einsum(
        "rwxyk,rkz->wxyz", back_x, back_tables, precision=lax.Precision.HIGHEST
    )
    mixed = jnp.dot(local_weight, lift_weight, precision=lax.Precision.HIGHEST)
    pre_act = (
        spectral_field
        + jnp.einsum("wc,cxyz->wxyz", mixed, fields, precision=lax.Precision.HIGHEST)
        + local_bias[:, None, None, None]
    )
    activated, gelu_back = jax.vjp(jax.nn.gelu, pre_act)
    predicted = jnp.einsum("w,wxyz->xyz", proj_weight, activated, precision=lax.Precision.HIGHEST)
    grad_pre = gelu_back(proj_weight[:, None, None, None] * cotangent[None])[0]
    field_sums = jnp.einsum("wxyz,cxyz->wc", grad_pre, fields, precision=lax.Precision.HIGHEST)
    proj_sums = jnp.einsum("wxyz,xyz->w", activated, cotangent, precision=lax.Precision.HIGHEST)
    field_sums, proj_sums = lax.psum((field_sums, proj_sums), ("gx", "gy"))
    grad_modes = spectral_forward(grad_pre, weights_z, 1.0 / total_x, 1.0 / total_y)
    grad_real = outer(grad_modes[0], spectrum[0]) + outer(grad_modes[1], spectrum[1])
    grad_imag = outer(grad_modes[1], spectrum[0]) - outer(grad_modes[0], spectrum[1])
    grad_spectral = jnp.stack([grad_real, grad_imag]).reshape(2, own_x, own_y, KZ, WIDTH * WIDTH)
    scale = 1.0 / math.sqrt(total_x * total_y * depth)
    grad_local = jnp.dot(field_sums, lift_weight.T, precision=lax.Precision.HIGHEST) * scale
    grad_proj = proj_sums * scale
    return (phase_next, solute_next, predicted, grad_spectral, grad_local, grad_proj)


def solution(mesh):
    return jax.shard_map(
        per_device,
        mesh=mesh,
        in_specs=(
            P("gx", "gy", None),
            P("gx", "gy", None),
            P("gx", "gy", None),
            P(),
            P(None, "gx", "gy", None, None),
            P(),
            P(),
            P(),
            P("gx", "gy", None),
        ),
        out_specs=(
            P("gx", "gy", None),
            P("gx", "gy", None),
            P("gx", "gy", None),
            P(None, "gx", "gy", None, None),
            P(),
            P(),
        ),
        check_vma=False,
    )
```

profile of v0, /device:TPU:1, one launch (start us, length us, event | category | flops | bytes accessed | tf_op | source)
XLA Modules:
  0.0 550.5 jit_solution(4324482883354596463)
XLA Ops:
  8.0 4.6 collective-permute-start
  12.6 6.1 %collective-permute-start.1 = (f32[2,1,8,256]{3,2,1,0:T(8,128)S(1)}, f32[2,1,8,256]{3,2,1,0:T(8,128)S(1)}, u32[]{:S(2)}, u32[]{:S(2)}) collective-permute-start(f32[2,1,8,256]{3,2,1,0:T(8,128)S(1)} %get-tuple-element.72), channel_id=1, source_target_pairs={{32,0},{64,32},{96,64},{128,96},{160,128},{192,160},{224,192},{256... | collective-permute-start | bytes 49160 | tf_op jit(solution)/shard_map/ppermute | solution.py:33
  20.5 2.8 collective-permute-start.2
  23.3 10.9 %collective-permute-start.3 = (f32[2,10,1,256]{3,2,1,0:T(1,128)S(1)}, f32[2,10,1,256]{3,2,1,0:T(1,128)S(1)}, u32[]{:S(2)}, u32[]{:S(2)}) collective-permute-start(f32[2,10,1,256]{3,2,1,0:T(1,128)S(1)} %get-tuple-element.66), channel_id=1, source_target_pairs={{1,0},{2,1},{3,2},{4,3},{5,4},{6,5},{7,6},{8,7},{9,8},{10,9},{11,1... | collective-permute-start | bytes 61448 | tf_op jit(solution)/shard_map/ppermute | solution.py:33
  36.7 2.8 collective-permute-start.4
  39.5 2.8 collective-permute-start.5
  46.8 7.5 %collective-permute-start.7 = (f32[2,10,1,256]{3,2,1,0:T(1,128)S(1)}, f32[2,10,1,256]{3,2,1,0:T(1,128)S(1)}, u32[]{:S(2)}, u32[]{:S(2)}) collective-permute-start(f32[2,10,1,256]{3,2,1,0:T(1,128)S(1)} %get-tuple-element.52), channel_id=1, source_target_pairs={{1,0},{2,1},{3,2},{4,3},{5,4},{6,5},{7,6},{8,7},{9,8},{10,9},{11,1... | collective-permute-start | bytes 61448 | tf_op jit(solution)/shard_map/ppermute | solution.py:33
  59.3 6.6 %fusion.36 = f32[2,32,8,8,32]{1,4,3,2,0:T(8,128)} fusion(f32[8,8,256,32]{2,3,1,0:T(8,128)S(1)} %fusion.263, f32[1,32,256]{2,1,0:T(8,128)S(1)} %get-tuple-element.84, f32[1,32,256]{2,1,0:T(8,128)S(1)} %get-tuple-element.83), kind=kOutput, calls=%fused_computation.41 | convolution fusion | flops 402669568 | bytes 2686976 | tf_op jit(solution)/shard_map/wxyz,rkz->rwxyk/dot_general | solution.py:173
  65.9 3.1 copy.66
  70.7 8.2 %all-to-all-start = ((f32[16,1,8192]{2,1,0:T(1,128)}), f32[16,1,8192]{2,1,0:T(1,128)S(1)}, u32[]{:S(2)}, u32[]{:S(2)}) async-start(f32[16,1,8192]{2,1,0:T(1,128)} %reshape.355), calls=%async_computation | async-start | bytes 1048576 | tf_op jit(solution)/shard_map/all_to_all | solution.py:115
  78.9 9.5 %all-to-all-done = f32[16,1,8192]{2,1,0:T(1,128)S(1)} async-done(((f32[16,1,8192]{2,1,0:T(1,128)}), f32[16,1,8192]{2,1,0:T(1,128)S(1)}, u32[]{:S(2)}, u32[]{:S(2)}) %all-to-all-start) | async-done | bytes 524320 | tf_op jit(solution)/shard_map/all_to_all | solution.py:115
  95.6 10.0 %all_to_all.126 = f32[16,1,2048]{2,1,0:T(1,128)S(1)} all-to-all(f32[16,1,2048]{2,1,0:T(1,128)S(1)} %reshape.357), channel_id=1, replica_groups=mesh['gx'=16,'gy'=32] {'gx'}, dimensions={0} | all-to-all | bytes 262144 | tf_op jit(solution)/shard_map/all_to_all | solution.py:124
  107.7 13.3 %all-to-all-start.2 = ((f32[32,1,1024]{2,1,0:T(1,128)}), f32[32,1,1024]{2,1,0:T(1,128)S(1)}, u32[]{:S(2)}, u32[]{:S(2)}) async-start(f32[32,1,1024]{2,1,0:T(1,128)} %reshape.359), calls=%async_computation.2 | async-start | bytes 262144 | tf_op jit(solution)/shard_map/all_to_all | solution.py:128
  121.8 14.0 %all-to-all-done.2 = f32[32,1,1024]{2,1,0:T(1,128)S(1)} async-done(((f32[32,1,1024]{2,1,0:T(1,128)}), f32[32,1,1024]{2,1,0:T(1,128)S(1)}, u32[]{:S(2)}, u32[]{:S(2)}) %all-to-all-start.2) | async-done | bytes 131104 | tf_op jit(solution)/shard_map/all_to_all | solution.py:128
  140.1 5.9 %all-to-all-start.3 = ((f32[32,1,128]{2,1,0:T(1,128)}), f32[32,1,128]{2,1,0:T(1,128)S(1)}, u32[]{:S(2)}, u32[]{:S(2)}) async-start(f32[32,1,128]{2,1,0:T(1,128)} %reshape.361), calls=%async_computation.3 | async-start | bytes 32768 | tf_op jit(solution)/shard_map/all_to_all | solution.py:137
  146.1 13.5 %all-to-all-done.3 = f32[32,1,128]{2,1,0:T(1,128)S(1)} async-done(((f32[32,1,128]{2,1,0:T(1,128)}), f32[32,1,128]{2,1,0:T(1,128)S(1)}, u32[]{:S(2)}, u32[]{:S(2)}) %all-to-all-start.3) | async-done | bytes 16416 | tf_op jit(solution)/shard_map/all_to_all | solution.py:137
  162.0 72.2 %all_gather.6 = f32[2,32,2,32,32]{4,1,2,0,3:T(8,128)S(1)} all-gather(f32[2,32,2,1,32]{4,1,2,0,3:T(8,128)S(1)} %pad_maximum_fusion.9), channel_id=1, replica_groups=mesh['gx'=16,'gy'=32] {'gy'}, dimensions={3}, use_global_device_ids=true | all-gather | bytes 540672 | tf_op jit(solution)/shard_map/all_gather | solution.py:187
  240.9 3.3 fusion.383
  244.1 62.8 %all-gather.2.cloned.1.call-done = f32[2,32,32,8,32]{4,3,2,1,0:T(8,128)} async-done(((f32[2,32,2,8,32]{4,3,2,1,0:T(8,128)}), f32[2,32,32,8,32]{4,3,2,1,0:T(8,128)}) %all-gather.2.cloned.1.call-update) | async-done | bytes 2097168 | tf_op jit(solution)/shard_map/all_gather | solution.py:192
  306.9 4.0 slice_bitcast_fusion.1
  313.6 2.8 fusion
  323.4 4.7 fusion.13
  329.5 7.6 %fusion.33 = f32[2,32,8,8,32]{1,4,3,2,0:T(8,128)} fusion(f32[32,8,8,256]{3,2,1,0:T(8,128)S(1)} %get-tuple-element.23, f32[1,32,256]{2,1,0:T(8,128)S(1)} %get-tuple-element.78, f32[1,32,256]{2,1,0:T(8,128)S(1)} %get-tuple-element.77), kind=kOutput, calls=%fused_computation.40 | convolution fusion | flops 402669568 | bytes 2686976 | tf_op jit(solution)/shard_map/wxyz,rkz->rwxyk/dot_general | solution.py:173
  337.1 3.8 copy.94
  343.4 14.6 %all_to_all.127 = f32[16,1,8192]{2,1,0:T(1,128)S(1)} all-to-all(f32[16,1,8192]{2,1,0:T(1,128)S(1)} %reshape.363), channel_id=1, replica_groups=mesh['gx'=16,'gy'=32] {'gx'}, dimensions={0} | all-to-all | bytes 1048576 | tf_op jit(solution)/shard_map/all_to_all | solution.py:115
  373.8 4.8 all-to-all-start.5
  381.4 3.3 all-to-all-done.5
  386.8 14.4 %all-to-all-start.6 = ((f32[32,1,1024]{2,1,0:T(1,128)}), f32[32,1,1024]{2,1,0:T(1,128)S(1)}, u32[]{:S(2)}, u32[]{:S(2)}) async-start(f32[32,1,1024]{2,1,0:T(1,128)} %reshape.367), calls=%async_computation.6 | async-start | bytes 262144 | tf_op jit(solution)/shard_map/all_to_all | solution.py:128
  401.2 4.3 fusion.69
  405.6 103.7 %all-reduce = (f32[32,2]{0,1:T(2,128)S(1)}, f32[32]{0:T(128)S(1)}) all-reduce(f32[32,2]{0,1:T(2,128)S(1)} %fusion.69, f32[32]{0:T(128)S(1)} %fusion.72), channel_id=1, replica_groups=mesh['gx'=16,'gy'=32] {'gx','gy'}, use_global_device_ids=true, to_apply=%region_0.1 | all-reduce | flops 96 | bytes 768 | tf_op jit(solution)/shard_map/psum | solution.py:212
  516.8 9.7 %all-to-all-start.7 = ((f32[32,1,128]{2,1,0:T(1,128)}), f32[32,1,128]{2,1,0:T(1,128)S(1)}, u32[]{:S(2)}, u32[]{:S(2)}) async-start(f32[32,1,128]{2,1,0:T(1,128)} %reshape.369), calls=%async_computation.7 | async-start | bytes 32768 | tf_op jit(solution)/shard_map/all_to_all | solution.py:137
  527.7 12.4 %all-to-all-done.7 = f32[32,1,128]{2,1,0:T(1,128)S(1)} async-done(((f32[32,1,128]{2,1,0:T(1,128)}), f32[32,1,128]{2,1,0:T(1,128)S(1)}, u32[]{:S(2)}, u32[]{:S(2)}) %all-to-all-start.7) | async-done | bytes 16416 | tf_op jit(solution)/shard_map/all_to_all | solution.py:137
  (197 shorter events, 85.3 us)
Async XLA Ops:
  7.2 233.4 %copy-start = (f32[32,32]{1,0:T(8,128)S(1)}, f32[32,32]{1,0:T(8,128)}, u32[]{:S(2)}) copy-start(f32[32,32]{1,0:T(8,128)} %param.14) | copy-start | bytes 12292
  7.2 29.2 %copy-start.3 = (f32[8,8,256]{2,1,0:T(8,128)S(1)}, f32[8,8,256]{2,1,0:T(8,128)}, u32[]{:S(2)}) copy-start(f32[8,8,256]{2,1,0:T(8,128)} %param.9) | copy-start | bytes 196612
  7.2 29.2 %copy-start.5 = (f32[8,8,256]{2,1,0:T(8,128)S(1)}, f32[8,8,256]{2,1,0:T(8,128)}, u32[]{:S(2)}) copy-start(f32[8,8,256]{2,1,0:T(8,128)} %param.10) | copy-start | bytes 196612
  7.2 29.2 %copy-start.14 = (f32[8,8,256]{2,1,0:T(8,128)S(1)}, f32[8,8,256]{2,1,0:T(8,128)}, u32[]{:S(2)}) copy-start(f32[8,8,256]{2,1,0:T(8,128)} %param.11) | copy-start | bytes 196612
  8.0 10.7 %collective-permute-start = (f32[2,1,8,256]{3,2,1,0:T(8,128)S(1)}, f32[2,1,8,256]{3,2,1,0:T(8,128)S(1)}, u32[]{:S(2)}, u32[]{:S(2)}) collective-permute-start(f32[2,1,8,256]{3,2,1,0:T(8,128)S(1)} %get-tuple-element.71), channel_id=1, source_target_pairs={{0,32},{32,64},{64,96},{96,128},{128,160},{160,192},{192,224},{224... | collective-permute-start | bytes 49160 | tf_op jit(solution)/shard_map/ppermute | solution.py:31
  12.6 6.9 %collective-permute-start.1 = (f32[2,1,8,256]{3,2,1,0:T(8,128)S(1)}, f32[2,1,8,256]{3,2,1,0:T(8,128)S(1)}, u32[]{:S(2)}, u32[]{:S(2)}) collective-permute-start(f32[2,1,8,256]{3,2,1,0:T(8,128)S(1)} %get-tuple-element.72), channel_id=1, source_target_pairs={{32,0},{64,32},{96,64},{128,96},{160,128},{192,160},{224,192},{256... | collective-permute-start | bytes 49160 | tf_op jit(solution)/shard_map/ppermute | solution.py:33
  20.5 13.7 %collective-permute-start.2 = (f32[2,10,1,256]{3,2,1,0:T(1,128)S(1)}, f32[2,10,1,256]{3,2,1,0:T(1,128)S(1)}, u32[]{:S(2)}, u32[]{:S(2)}) collective-permute-start(f32[2,10,1,256]{3,2,1,0:T(1,128)S(1)} %get-tuple-element.65), channel_id=1, source_target_pairs={{0,1},{1,2},{2,3},{3,4},{4,5},{5,6},{6,7},{7,8},{8,9},{9,10},{10,1... | collective-permute-start | bytes 61448 | tf_op jit(solution)/shard_map/ppermute | solution.py:31
  23.3 11.7 %collective-permute-start.3 = (f32[2,10,1,256]{3,2,1,0:T(1,128)S(1)}, f32[2,10,1,256]{3,2,1,0:T(1,128)S(1)}, u32[]{:S(2)}, u32[]{:S(2)}) collective-permute-start(f32[2,10,1,256]{3,2,1,0:T(1,128)S(1)} %get-tuple-element.66), channel_id=1, source_target_pairs={{1,0},{2,1},{3,2},{4,3},{5,4},{6,5},{7,6},{8,7},{9,8},{10,9},{11,1... | collective-permute-start | bytes 61448 | tf_op jit(solution)/shard_map/ppermute | solution.py:33
  36.7 5.7 %collective-permute-start.4 = (f32[2,1,8,256]{3,2,1,0:T(8,128)S(1)}, f32[2,1,8,256]{3,2,1,0:T(8,128)S(1)}, u32[]{:S(2)}, u32[]{:S(2)}) collective-permute-start(f32[2,1,8,256]{3,2,1,0:T(8,128)S(1)} %get-tuple-element.69), channel_id=1, source_target_pairs={{0,32},{32,64},{64,96},{96,128},{128,160},{160,192},{192,224},{224... | collective-permute-start | bytes 49160 | tf_op jit(solution)/shard_map/ppermute | solution.py:31
  39.5 5.4 collective-permute-start.5
  44.9 9.6 %collective-permute-start.6 = (f32[2,10,1,256]{3,2,1,0:T(1,128)S(1)}, f32[2,10,1,256]{3,2,1,0:T(1,128)S(1)}, u32[]{:S(2)}, u32[]{:S(2)}) collective-permute-start(f32[2,10,1,256]{3,2,1,0:T(1,128)S(1)} %get-tuple-element.51), channel_id=1, source_target_pairs={{0,1},{1,2},{2,3},{3,4},{4,5},{5,6},{6,7},{7,8},{8,9},{9,10},{10,1... | collective-permute-start | bytes 61448 | tf_op jit(solution)/shard_map/ppermute | solution.py:31
  46.8 8.4 %collective-permute-start.7 = (f32[2,10,1,256]{3,2,1,0:T(1,128)S(1)}, f32[2,10,1,256]{3,2,1,0:T(1,128)S(1)}, u32[]{:S(2)}, u32[]{:S(2)}) collective-permute-start(f32[2,10,1,256]{3,2,1,0:T(1,128)S(1)} %get-tuple-element.52), channel_id=1, source_target_pairs={{1,0},{2,1},{3,2},{4,3},{5,4},{6,5},{7,6},{8,7},{9,8},{10,9},{11,1... | collective-permute-start | bytes 61448 | tf_op jit(solution)/shard_map/ppermute | solution.py:33
  55.3 2.1 copy-start.17
  70.7 17.7 %all-to-all-start = ((f32[16,1,8192]{2,1,0:T(1,128)}), f32[16,1,8192]{2,1,0:T(1,128)S(1)}, u32[]{:S(2)}, u32[]{:S(2)}) async-start(f32[16,1,8192]{2,1,0:T(1,128)} %reshape.355), calls=%async_computation | async-start | bytes 1048576 | tf_op jit(solution)/shard_map/all_to_all | solution.py:115
  78.9 240.3 %copy-start.11 = (s32[32]{0:T(128)}, s32[32]{0:T(128)S(1)}, u32[]{:S(2)}) copy-start(s32[32]{0:T(128)S(1)} %compare_select_fusion) | copy-start | bytes 388
  95.6 25.4 %copy-start.6 = (f32[2,2,1,32,1024]{4,3,2,1,0:T(8,128)S(1)}, f32[2,2,1,32,1024]{4,3,2,1,0:T(8,128)}, u32[]{:S(2)}) copy-start(f32[2,2,1,32,1024]{4,3,2,1,0:T(8,128)} %param.13) | copy-start | bytes 1572868
  107.7 28.1 %all-to-all-start.2 = ((f32[32,1,1024]{2,1,0:T(1,128)}), f32[32,1,1024]{2,1,0:T(1,128)S(1)}, u32[]{:S(2)}, u32[]{:S(2)}) async-start(f32[32,1,1024]{2,1,0:T(1,128)} %reshape.359), calls=%async_computation.2 | async-start | bytes 262144 | tf_op jit(solution)/shard_map/all_to_all | solution.py:128
  140.1 19.4 %all-to-all-start.3 = ((f32[32,1,128]{2,1,0:T(1,128)}), f32[32,1,128]{2,1,0:T(1,128)S(1)}, u32[]{:S(2)}, u32[]{:S(2)}) async-start(f32[32,1,128]{2,1,0:T(1,128)} %reshape.361), calls=%async_computation.3 | async-start | bytes 32768 | tf_op jit(solution)/shard_map/all_to_all | solution.py:137
  146.0 160.9 %all-gather.2.cloned.1.call-start = ((), (), s32[]{:S(2)}) async-start(), calls=%async_computation.8 | async-start | bytes 8912896 | tf_op jit(solution)/shard_map/all_gather | solution.py:192
  160.4 73.8 %copy-start.7 = (f32[2,32,32]{2,1,0:T(8,128)}, f32[2,32,32]{2,1,0:T(8,128)S(1)}, u32[]{:S(2)}) copy-start(f32[2,32,32]{2,1,0:T(8,128)S(1)} %copy.178) | copy-start | bytes 24580
  160.5 73.7 %copy-start.9 = (f32[2,32,32]{2,1,0:T(8,128)}, f32[2,32,32]{2,1,0:T(8,128)S(1)}, u32[]{:S(2)}) copy-start(f32[2,32,32]{2,1,0:T(8,128)S(1)} %copy.179) | copy-start | bytes 24580
  321.8 1.6 copy-start.4
  321.8 1.6 copy-start.15
  372.3 6.3 %copy-start.16 = (f32[8,8,256]{2,1,0:T(8,128)S(1)}, f32[8,8,256]{2,1,0:T(8,128)}, u32[]{:S(2)}) copy-start(f32[8,8,256]{2,1,0:T(8,128)} %param.17) | copy-start | bytes 196612
  373.8 10.9 %all-to-all-start.5 = ((f32[16,1,2048]{2,1,0:T(1,128)}), f32[16,1,2048]{2,1,0:T(1,128)S(1)}, u32[]{:S(2)}, u32[]{:S(2)}) async-start(f32[16,1,2048]{2,1,0:T(1,128)} %reshape.365), calls=%async_computation.5 | async-start | bytes 262144 | tf_op jit(solution)/shard_map/all_to_all | solution.py:124
  385.8 123.4 %copy-start.18 = (f32[32,2]{0,1:T(2,128)S(1)}, f32[32,2]{0,1:T(2,128)}, u32[]{:S(2)}) copy-start(f32[32,2]{0,1:T(2,128)} %param.12) | copy-start | bytes 772
  385.8 124.3 %copy-start.20 = (f32[32]{0:T(128)S(1)}, f32[32]{0:T(128)}, u32[]{:S(2)}) copy-start(f32[32]{0:T(128)} %param.16) | copy-start | bytes 388
  386.8 125.6 %all-to-all-start.6 = ((f32[32,1,1024]{2,1,0:T(1,128)}), f32[32,1,1024]{2,1,0:T(1,128)S(1)}, u32[]{:S(2)}, u32[]{:S(2)}) async-start(f32[32,1,1024]{2,1,0:T(1,128)} %reshape.367), calls=%async_computation.6 | async-start | bytes 262144 | tf_op jit(solution)/shard_map/all_to_all | solution.py:128
  513.5 27.5 %copy-start.8 = (f32[2,32,32]{2,1,0:T(8,128)S(1)}, f32[2,32,32]{2,1,0:T(8,128)}, u32[]{:S(2)}) copy-start(f32[2,32,32]{2,1,0:T(8,128)} %copy-done.7) | copy-start | bytes 24580
  513.5 27.5 %copy-start.10 = (f32[2,32,32]{2,1,0:T(8,128)S(1)}, f32[2,32,32]{2,1,0:T(8,128)}, u32[]{:S(2)}) copy-start(f32[2,32,32]{2,1,0:T(8,128)} %copy-done.9) | copy-start | bytes 24580
  516.8 23.2 %all-to-all-start.7 = ((f32[32,1,128]{2,1,0:T(1,128)}), f32[32,1,128]{2,1,0:T(1,128)S(1)}, u32[]{:S(2)}, u32[]{:S(2)}) async-start(f32[32,1,128]{2,1,0:T(1,128)} %reshape.369), calls=%async_computation.7 | async-start | bytes 32768 | tf_op jit(solution)/shard_map/all_to_all | solution.py:137
  541.0 2.4 copy-start.1
  (5 other events, 5.8 us)
Sparse Core Ops, SparseCore 0:
  240.6 66.2 all-gather.1
where the time goes:
time: 558 us; the launch traced here: 551 us
  blocking collectives  200 us (36%)
  waiting for transfers between devices  120 us (22%)
  starting transfers between devices  95.8 us (17%)
  matrix products  61.8 us (11%)
  local copies, waits for them, and re-layouts  39.9 us (7%)
  other arithmetic  16.9 us (3%)
  between operations  15.3 us (3%)
    psum x1, blocking collectives, per_device(): field_sums, proj_sums = lax.psum((field_sums, proj_sums), ('gx', 'gy'))  104 us
    all_gather x1, blocking collectives, per_device(): portion = lax.all_gather(spectral_out, 'gy', axis=3, tiled=True)  72.2 us
    all_gather x1, waiting for transfers between devices, per_device(): portion = lax.all_gather(back_y, 'gx', axis=2, tiled=True)  62.8 us
    all_to_all x2, starting transfers between devices, y_forward(): lax.all_to_all(data, 'gy', split_axis=1, concat_axis=3, tiled=True)  27.7 us
    dot_general x24, matrix products, apply(): return jnp.einsum(pattern, table, values, precision=lax.Precision.HIGHEST)  27.4 us
    ppermute x4, starting transfers between devices, extended(): lax.ppermute(head, axis, [((i + 1) % count, i) for i in range(count)])  27.3 us
    all_to_all x2, waiting for transfers between devices, y_forward(): return lax.all_to_all(lines, 'gy', split_axis=3, concat_axis=1, tiled=True)  25.8 us
    unnamed x63, local copies, waits for them, and re-layouts  15.9 us
  transfers between devices with their start and end apart: 15, of which 10 were waited for; matrix products, arithmetic and copies ran while one was open for 3% of the time, Pallas kernels for 0%

commit v1 on v0

v1 whole, which is shorter than its diff:
```python
import math

import numpy as np

import jax
import jax.numpy as jnp
from jax import lax
from jax.sharding import PartitionSpec as P

TIME_STEP = 0.05
COUPLING = 2.0
SOLID_DIFF = 0.05
LIQUID_DIFF = 1.0
PARTITION = 0.15
TRAP_RATE = 4.0
SOLUTE_MEAN = 0.5
GELU_K = math.sqrt(2.0 / math.pi)
GELU_C = 0.044715
F32 = jnp.float32


def mm(a, b):
    return jnp.dot(a, b, precision=lax.Precision.HIGH, preferred_element_type=F32)


def signed(count):
    index = np.arange(count)
    return np.where(index < count // 2, index, index - count)


def trig(freqs, places, length, factor=1.0):
    angle = 2.0 * np.pi * ((freqs[:, None] * places[None, :]) % length) / length
    return np.cos(angle) * factor, np.sin(angle) * factor


def z_tables(modes, depth):
    cos, sin = trig(np.arange(modes), np.arange(depth), depth)
    lanes = 2 * modes
    weight = np.where(np.arange(modes) == 0, 1.0, 2.0) / depth
    both = np.stack([cos, -sin])

    def blocks(one):
        full = np.zeros((2 * depth, 2 * lanes))
        full[:depth, :lanes] = one
        full[depth:, lanes:] = one
        return full

    plain = both.reshape(lanes, depth).T
    heavy = (both * weight[None, :, None]).reshape(lanes, depth).T
    return blocks(plain), blocks(heavy), blocks(heavy).T


def rot(v, quarter):
    lane = lax.broadcasted_iota(jnp.int32, v.shape, v.ndim - 1)
    imag = (lane // quarter) % 2 == 1
    return jnp.where(imag, -jnp.roll(v, quarter, v.ndim - 1), jnp.roll(v, -quarter, v.ndim - 1))


def diffusivity(phase_now):
    return SOLID_DIFF + (LIQUID_DIFF - SOLID_DIFF) * 0.5 * (1.0 - jnp.tanh(phase_now))


def around(f):
    centre = f[1:-1, 1:-1]
    return [
        f[2:, 1:-1],
        f[:-2, 1:-1],
        f[1:-1, 2:],
        f[1:-1, :-2],
        jnp.roll(centre, -1, 2),
        jnp.roll(centre, 1, 2),
    ]


def sweep(phase, solute, undercool):
    diff = diffusivity(phase)
    p, c, d = phase[1:-1, 1:-1], solute[1:-1, 1:-1], diff[1:-1, 1:-1]
    lap = sum(around(phase)) - 6.0 * p
    squares = 1.0 - p * p
    rate = lap + p - p * p * p + COUPLING * squares * squares * (undercool - c)
    div = sum(0.5 * (d + dn) * (cn - c) for dn, cn in zip(around(diff), around(solute)))
    speed = TRAP_RATE * jnp.abs(rate)
    keff = (PARTITION + speed) / (1.0 + speed)
    return p + TIME_STEP * rate, c + TIME_STEP * (div + 0.5 * (1.0 - keff) * c * rate)


def extended(cells, axis, dim, width):
    count = lax.axis_size(axis)
    head = lax.slice_in_dim(cells, 0, width, axis=dim)
    tail = lax.slice_in_dim(cells, cells.shape[dim] - width, cells.shape[dim], axis=dim)
    up = lax.ppermute(tail, axis, [(i, (i + 1) % count) for i in range(count)])
    down = lax.ppermute(head, axis, [((i + 1) % count, i) for i in range(count)])
    return jnp.concatenate([up, cells, down], axis=dim)


def swap(data, axis):
    shape = data.shape
    flat = data.reshape(shape[0], -1)
    return lax.all_to_all(flat, axis, split_axis=0, concat_axis=0, tiled=True).reshape(shape)


def per_device(phase, solute, undercool, lift, weight, local_weight, bias, proj, cotangent):
    gx, gy = lax.axis_size("gx"), lax.axis_size("gy")
    ix, iy = lax.axis_index("gx"), lax.axis_index("gy")
    cx, cy, depth = phase.shape
    own_kx, own_ky, kz = weight.shape[1:4]
    width = lift.shape[0]
    nx, ny, kx, ky = gx * cx, gy * cy, gx * own_kx, gy * own_ky
    pairs = width // 2
    assert pairs == gx and pairs * own_kx == gy and own_ky == 1
    lanes = 4 * kz
    fx, fy = signed(kx), signed(ky)
    zf, zg, zi = (jnp.asarray(t, F32) for t in z_tables(kz, depth))
    cosx, sinx = trig(fx, np.arange(nx), nx)
    cosy, siny = trig(fy, np.arange(ny), ny)

    def own(cos, sin, count, size, at):
        both = np.concatenate([cos, sin]).reshape(-1, count, size).transpose(1, 0, 2)
        return jnp.asarray(both, F32)[at]

    stack = jnp.stack([phase, solute, undercool])
    stack = extended(extended(stack, "gx", 1, 2), "gy", 2, 2)
    mid_p, mid_c = sweep(stack[0], stack[1], stack[2, 1:-1, 1:-1])
    phase_next, solute_next = sweep(mid_p, mid_c, undercool)

    pf = jnp.swapaxes(phase_next, 0, 1).reshape(cy * cx, depth)
    cf = jnp.swapaxes(solute_next - SOLUTE_MEAN, 0, 1).reshape(cy * cx, depth)
    along = mm(jnp.concatenate([pf, cf], 1), zf).reshape(cy, cx, lanes)
    wave = jnp.einsum("kx,yxl->kyl", own(cosx, sinx, gx, cx, ix), along, precision=lax.Precision.HIGH)
    wave = wave[:kx] + rot(wave[kx:], kz)
    got = swap(wave.reshape(gx, own_kx, cy, lanes), "gx").sum(0)
    wave = jnp.einsum("ky,xyl->kxl", own(cosy, siny, gy, cy, iy), got, precision=lax.Precision.HIGH)
    wave = wave[:ky] + rot(wave[ky:], kz)
    spec = swap(wave.reshape(gy, own_kx, lanes), "gy").sum(0)
    spec = spec.reshape(own_kx, 2, 2, kz)

    shaped = weight.reshape(2, own_kx, kz, width, width)
    both = jnp.einsum("rxzoi,ic->rxcoz", shaped, lift, precision=lax.Precision.HIGH)
    re, im = spec[:, :, 0, None, :], spec[:, :, 1, None, :]
    out_re = (both[0] * re - both[1] * im).sum(1)
    out_im = (both[0] * im + both[1] * re).sum(1)
    out = jnp.stack([out_re, out_im], 2).reshape(own_kx, 2, pairs, 2, kz)
    out = out.transpose(2, 0, 1, 3, 4).reshape(gy, lanes)

    got = swap(out, "gy")
    table = jnp.asarray(np.concatenate([cosy, -siny]).T / ny, F32)
    lines = mm(table, jnp.concatenate([got, rot(got, kz)], 0))
    got = swap(lines.reshape(gy, cy, lanes), "gy")
    got = swap(got.reshape(gx, own_kx, cy, lanes), "gx").reshape(kx, cy * lanes)
    turned = rot(got.reshape(kx, cy, lanes), kz).reshape(kx, cy * lanes)
    table = jnp.asarray(np.concatenate([cosx, -sinx]).T / nx, F32)
    lines = mm(table, jnp.concatenate([got, turned], 0))
    lines = lines.reshape(gx, cx, cy, lanes).transpose(0, 2, 1, 3)
    got = swap(lines, "gx").reshape(pairs * cy * cx, lanes)
    field = mm(got, zi).reshape(pairs, cy * cx, 2, depth)

    mixed = jnp.dot(local_weight, lift, precision=lax.Precision.HIGHEST)

    def per_channel(v):
        return v.reshape(2, pairs).T[:, None, :, None]

    pre = field + per_channel(mixed[:, 0]) * pf[:, None] + per_channel(mixed[:, 1]) * cf[:, None] + per_channel(bias)
    cot = jnp.swapaxes(cotangent, 0, 1).reshape(cy * cx, 1, depth)
    square = pre * pre
    tanh = jnp.tanh(GELU_K * (pre + GELU_C * (square * pre)))
    half = 0.5 * (1.0 + tanh)
    act = pre * half
    slope = half + 0.5 * GELU_K * pre * (1.0 - tanh * tanh) * (1.0 + 3.0 * GELU_C * square)
    predicted = (per_channel(proj) * act).sum((0, 2)).reshape(cy, cx, depth)
    predicted = jnp.swapaxes(predicted, 0, 1)
    grad = per_channel(proj) * cot * slope
    sums = jnp.stack(
        [(grad * pf[:, None]).sum((1, 3)), (grad * cf[:, None]).sum((1, 3)), (act * cot).sum((1, 3))]
    )

    along = mm(grad.reshape(pairs * cy * cx, 2 * depth), zg).reshape(gx, cy, cx, lanes)
    got = swap(along, "gx").transpose(0, 2, 1, 3).reshape(nx, cy * lanes)
    wave = mm(jnp.asarray(np.concatenate([cosx, sinx]) / nx, F32), got).reshape(2, kx, cy, lanes)
    wave = wave[0] + rot(wave[1], kz)
    row = jnp.pad(sums.reshape(-1), (0, lanes - 3 * width)) if lanes >= 3 * width else sums.reshape(-1)
    row = jnp.pad(row.reshape(1, lanes), ((0, cy - 1), (0, 0)))
    wave = jnp.concatenate([wave.reshape(gx, own_kx * cy, lanes), jnp.broadcast_to(row, (gx, cy, lanes))], 1)
    got = swap(wave, "gx")
    row = got[:, own_kx * cy].sum(0)
    got = swap(got[:, : own_kx * cy].reshape(gy, cy, lanes), "gy").reshape(ny, lanes)
    wave = mm(jnp.asarray(np.concatenate([cosy, siny]) / ny, F32), got)
    wave = wave[:ky] + rot(wave[ky:], kz)
    wave = jnp.stack([wave, jnp.broadcast_to(row, (gy, lanes))], 1)
    got = swap(wave, "gy")
    sums = got[:, 1].sum(0)[: 3 * width].reshape(3, pairs, 2).transpose(0, 2, 1).reshape(3, width)
    modes = got[:, 0].reshape(pairs, own_kx, 2, 2, kz).transpose(3, 1, 4, 2, 0).reshape(2, own_kx, kz, width)

    source = jnp.einsum("xcrz,ic->rxzi", spec, lift, precision=lax.Precision.HIGH)
    g, s = modes[:, :, :, :, None], source[:, :, :, None, :]
    grad_spectral = jnp.stack([g[0] * s[0] + g[1] * s[1], g[1] * s[0] - g[0] * s[1]])
    grad_spectral = grad_spectral.reshape(2, own_kx, 1, kz, width * width)
    scale = 1.0 / math.sqrt(nx * ny * depth)
    grad_local = jnp.dot(sums[:2].T, lift.T, precision=lax.Precision.HIGHEST) * scale
    return phase_next, solute_next, predicted, grad_spectral, grad_local, sums[2] * scale


def solution(mesh):
    tile, modes = P("gx", "gy", None), P(None, "gx", "gy", None, None)
    return jax.shard_map(
        per_device,
        mesh=mesh,
        in_specs=(tile, tile, tile, P(), modes, P(), P(), P(), tile),
        out_specs=(tile, tile, tile, modes, P(), P()),
        check_vma=False,
    )
```

time: 558 us -> 225 us (0.40); the launches traced: 551 us -> 223 us
  blocking collectives: 200 us -> 28.2 us
  matrix products: 61.8 us -> 15 us
  waiting for transfers between devices: 120 us -> 83 us
  starting transfers between devices: 95.8 us -> 73.4 us
  local copies, waits for them, and re-layouts: 39.9 us -> 18 us
  between operations: 15.3 us -> 1.45 us
  other arithmetic: 16.9 us -> 4.03 us
    psum x1 -> x0, blocking collectives: 104 us -> none  [per_device(): field_sums, proj_sums = lax.psum((field_sums, proj_sums), ('gx', 'gy'))]
    all_gather x1 -> x0, blocking collectives: 72.2 us -> none  [per_device(): portion = lax.all_gather(spectral_out, 'gy', axis=3, tiled=True)]
    all_gather x1 -> x0, waiting for transfers between devices: 62.8 us -> none  [per_device(): portion = lax.all_gather(back_y, 'gx', axis=2, tiled=True)]
    dot_general x34 -> x16, matrix products: 61.8 us -> 15 us  [the longest x10 7.68 us: mm(): jnp.dot(a, b, precision=lax.Precision.HIGH, preferred_element_type=F32)]
    all_to_all x6 -> x8, waiting for transfers between devices: 52.7 us -> 80.6 us  [swap(): lax.all_to_all(flat, axis, split_axis=0, concat_axis=0, tiled=True)]
    unnamed x63 -> x43, local copies, waits for them, and re-layouts: 15.9 us -> 4.16 us
    ppermute x4 -> x2, starting transfers between devices: 27.3 us -> 16.9 us  [extended(): lax.ppermute(head, axis, [((i + 1) % count, i) for i in range(count)])]
    all_to_all x8 -> x1, other arithmetic: 8.26 us -> 0.31 us  [swap(): lax.all_to_all(flat, axis, split_axis=0, concat_axis=0, tiled=True)]
  transfers between devices with their start and end apart: 15 -> 12, of which waited for: 10 -> 11; matrix products, arithmetic and copies ran while one was open for 3% -> 4% of each run, Pallas kernels for 0% -> 0%
where the time goes in v1:
time: 225 us; the launch traced here: 223 us
  waiting for transfers between devices  83 us (37%)
  starting transfers between devices  73.4 us (33%)
  blocking collectives  28.2 us (13%)
  local copies, waits for them, and re-layouts  18 us (8%)
  matrix products  15 us (7%)
  other arithmetic  4.03 us (2%)
    all_to_all x8, waiting for transfers between devices, swap(): lax.all_to_all(flat, axis, split_axis=0, concat_axis=0, tiled=True)  80.6 us
    all_to_all x8, starting transfers between devices, swap(): lax.all_to_all(flat, axis, split_axis=0, concat_axis=0, tiled=True)  48.8 us
    all_to_all x2, blocking collectives, swap(): lax.all_to_all(flat, axis, split_axis=0, concat_axis=0, tiled=True)  28.2 us
    ppermute x2, starting transfers between devices, extended(): lax.ppermute(head, axis, [((i + 1) % count, i) for i in range(count)])  16.9 us
    ppermute x2, starting transfers between devices, extended(): up = lax.ppermute(tail, axis, [(i, (i + 1) % count) for i in range(count)])  7.69 us
    dot_general x10, matrix products, mm(): jnp.dot(a, b, precision=lax.Precision.HIGH, preferred_element_type=F32)  7.68 us
  transfers between devices with their start and end apart: 12, of which 11 were waited for; matrix products, arithmetic and copies ran while one was open for 4% of the time, Pallas kernels for 0%

profile of v1, /device:TPU:1, one launch (start us, length us, event | category | flops | bytes accessed | tf_op | source)
XLA Modules:
  0.0 223.1 jit_solution(4094234703213945124)
XLA Ops:
  0.6 0.9 copy.222
  1.5 0.9 copy_bitcast_fusion.1
  2.5 4.6 %collective-permute-start = (f32[3,2,8,256]{3,1,2,0:T(2,128)S(1)}, f32[3,2,8,256]{3,1,2,0:T(2,128)S(1)}, u32[]{:S(2)}, u32[]{:S(2)}) collective-permute-start(f32[3,2,8,256]{3,1,2,0:T(2,128)S(1)} %get-tuple-element.67), channel_id=1, source_target_pairs={{0,32},{32,64},{64,96},{96,128},{128,160},{160,192},{192,224},{224... | collective-permute-start | bytes 147464 | tf_op jit(solution)/shard_map/ppermute | solution.py:91
  7.1 6.1 %collective-permute-start.1 = (f32[3,2,8,256]{3,1,2,0:T(2,128)S(1)}, f32[3,2,8,256]{3,1,2,0:T(2,128)S(1)}, u32[]{:S(2)}, u32[]{:S(2)}) collective-permute-start(f32[3,2,8,256]{3,1,2,0:T(2,128)S(1)} %get-tuple-element.68), channel_id=1, source_target_pairs={{32,0},{64,32},{96,64},{128,96},{160,128},{192,160},{224,192},{256... | collective-permute-start | bytes 147464 | tf_op jit(solution)/shard_map/ppermute | solution.py:92
  14.1 3.1 %collective-permute-start.2 = (f32[3,12,2,256]{3,1,2,0:T(8,128)S(1)}, f32[3,12,2,256]{3,1,2,0:T(8,128)S(1)}, u32[]{:S(2)}, u32[]{:S(2)}) collective-permute-start(f32[3,12,2,256]{3,1,2,0:T(8,128)S(1)} %get-tuple-element.47), channel_id=1, source_target_pairs={{0,1},{1,2},{2,3},{3,4},{4,5},{5,6},{6,7},{7,8},{8,9},{9,10},{10,1... | collective-permute-start | bytes 221192 | tf_op jit(solution)/shard_map/ppermute | solution.py:91
  17.2 10.9 %collective-permute-start.3 = (f32[3,12,2,256]{3,1,2,0:T(8,128)S(1)}, f32[3,12,2,256]{3,1,2,0:T(8,128)S(1)}, u32[]{:S(2)}, u32[]{:S(2)}) collective-permute-start(f32[3,12,2,256]{3,1,2,0:T(8,128)S(1)} %get-tuple-element.48), channel_id=1, source_target_pairs={{1,0},{2,1},{3,2},{4,3},{5,4},{6,5},{7,6},{8,7},{9,8},{10,9},{11,1... | collective-permute-start | bytes 221192 | tf_op jit(solution)/shard_map/ppermute | solution.py:92
  28.2 1.5 collective-permute-done.3
  32.4 1.0 fusion.106
  34.5 5.8 %all-to-all-start = ((f32[16,1,2048]{2,1,0:T(1,128)}), f32[16,1,2048]{2,1,0:T(1,128)S(1)}, u32[]{:S(2)}, u32[]{:S(2)}) async-start(f32[16,1,2048]{2,1,0:T(1,128)} %bitcast.20), calls=%async_computation | async-start | bytes 262144 | tf_op jit(solution)/shard_map/all_to_all | solution.py:99
  41.0 5.4 %all-to-all-done = f32[16,1,2048]{2,1,0:T(1,128)S(1)} async-done(((f32[16,1,2048]{2,1,0:T(1,128)}), f32[16,1,2048]{2,1,0:T(1,128)S(1)}, u32[]{:S(2)}, u32[]{:S(2)}) %all-to-all-start) | async-done | bytes 131104 | tf_op jit(solution)/shard_map/all_to_all | solution.py:99
  46.5 0.9 fusion.103
  48.4 13.0 %all-to-all-start.1 = ((f32[32,1,256]{2,1,0:T(1,128)}), f32[32,1,256]{2,1,0:T(1,128)S(1)}, u32[]{:S(2)}, u32[]{:S(2)}) async-start(f32[32,1,256]{2,1,0:T(1,128)} %bitcast.22), calls=%async_computation.1 | async-start | bytes 65536 | tf_op jit(solution)/shard_map/all_to_all | solution.py:99
  61.3 4.1 %convolution_bitcast_fusion = f32[2,2,2,32,32]{3,2,4,1,0:T(2,128)S(1)} fusion(f32[2,2,32,32,32]{4,3,2,1,0:T(8,128)S(1)} %reshape.276, f32[32,2]{0,1:T(2,128)S(1)} %copy-done.13), kind=kOutput, calls=%fused_computation.21 | convolution fusion | flops 1572864 | bytes 557312 | tf_op jit(solution)/shard_map/rxzoi,ic->rxcoz/dot_general | solution.py:138
  65.5 9.6 %all-to-all-done.1 = f32[32,1,256]{2,1,0:T(1,128)S(1)} async-done(((f32[32,1,256]{2,1,0:T(1,128)}), f32[32,1,256]{2,1,0:T(1,128)S(1)}, u32[]{:S(2)}, u32[]{:S(2)}) %all-to-all-start.1) | async-done | bytes 32800 | tf_op jit(solution)/shard_map/all_to_all | solution.py:99
  76.1 17.8 %all_to_all.93 = f32[32,1,128]{2,1,0:T(1,128)S(1)} all-to-all(f32[32,1,128]{2,1,0:T(1,128)S(1)} %bitcast.234), channel_id=1, replica_groups=mesh['gx'=16,'gy'=32] {'gy'}, dimensions={0} | all-to-all | bytes 32768 | tf_op jit(solution)/shard_map/all_to_all | solution.py:99
  95.4 4.6 %all-to-all-start.3 = ((f32[32,1,1024]{2,1,0:T(1,128)}), f32[32,1,1024]{2,1,0:T(1,128)}, u32[]{:S(2)}, u32[]{:S(2)}) async-start(f32[32,1,1024]{2,1,0:T(1,128)} %bitcast.32), calls=%async_computation.3 | async-start | bytes 262144 | tf_op jit(solution)/shard_map/all_to_all | solution.py:99
  100.0 14.7 %all-to-all-done.3 = f32[32,1,1024]{2,1,0:T(1,128)} async-done(((f32[32,1,1024]{2,1,0:T(1,128)}), f32[32,1,1024]{2,1,0:T(1,128)}, u32[]{:S(2)}, u32[]{:S(2)}) %all-to-all-start.3) | async-done | bytes 131104 | tf_op jit(solution)/shard_map/all_to_all | solution.py:99
  114.8 7.2 %all-to-all-start.4 = ((f32[16,1,2048]{2,1,0:T(1,128)}), f32[16,1,2048]{2,1,0:T(1,128)S(1)}, u32[]{:S(2)}, u32[]{:S(2)}) async-start(f32[16,1,2048]{2,1,0:T(1,128)} %bitcast.33), calls=%async_computation.4 | async-start | bytes 262144 | tf_op jit(solution)/shard_map/all_to_all | solution.py:99
  122.0 6.2 %all-to-all-done.4 = f32[16,1,2048]{2,1,0:T(1,128)S(1)} async-done(((f32[16,1,2048]{2,1,0:T(1,128)}), f32[16,1,2048]{2,1,0:T(1,128)S(1)}, u32[]{:S(2)}, u32[]{:S(2)}) %all-to-all-start.4) | async-done | bytes 131104 | tf_op jit(solution)/shard_map/all_to_all | solution.py:99
  130.5 0.9 copy.170
  131.4 4.0 %all-to-all-start.5 = ((f32[16,1,8192]{2,1,0:T(1,128)}), f32[16,1,8192]{2,1,0:T(1,128)S(1)}, u32[]{:S(2)}, u32[]{:S(2)}) async-start(f32[16,1,8192]{2,1,0:T(1,128)} %bitcast.40), calls=%async_computation.5 | async-start | bytes 1048576 | tf_op jit(solution)/shard_map/all_to_all | solution.py:99
  136.3 8.9 %all-to-all-done.5 = f32[16,1,8192]{2,1,0:T(1,128)S(1)} async-done(((f32[16,1,8192]{2,1,0:T(1,128)}), f32[16,1,8192]{2,1,0:T(1,128)S(1)}, u32[]{:S(2)}, u32[]{:S(2)}) %all-to-all-start.5) | async-done | bytes 524320 | tf_op jit(solution)/shard_map/all_to_all | solution.py:99
  145.2 3.3 %multiply_reduce_fusion.2 = (f32[16,2]{1,0:T(8,128)S(1)}, f32[16,2]{1,0:T(8,128)S(1)}, f32[16,64,2,256]{3,1,2,0:T(8,128)S(1)}, f32[64,256]{1,0:T(8,128)S(1)}, f32[16,2]{1,0:T(8,128)S(1)}) fusion(f32[64,256]{1,0:T(8,128)S(1)} %bitcast.213, f32[64,256]{1,0:T(8,128)S(1)} %get-tuple-element.39, f32[64,256]{1,0:T(8,128)S(1)} %bitcast.236, ...), kind=kOutput, calls=%fused_computation.12 | convolution fusion | flops 418889632 | bytes 3146624 | tf_op jit(solution)/shard_map/dot_general | solution.py:23
  148.5 1.6 copy.176
  151.1 1.8 fusion.158
  152.9 4.6 %all-to-all-start.6 = ((f32[16,1,8192]{2,1,0:T(1,128)}), f32[16,1,8192]{2,1,0:T(1,128)S(1)}, u32[]{:S(2)}, u32[]{:S(2)}) async-start(f32[16,1,8192]{2,1,0:T(1,128)} %bitcast.54), calls=%async_computation.6 | async-start | bytes 1048576 | tf_op jit(solution)/shard_map/all_to_all | solution.py:99
  158.0 9.3 %all-to-all-done.6 = f32[16,1,8192]{2,1,0:T(1,128)S(1)} async-done(((f32[16,1,8192]{2,1,0:T(1,128)}), f32[16,1,8192]{2,1,0:T(1,128)S(1)}, u32[]{:S(2)}, u32[]{:S(2)}) %all-to-all-start.6) | async-done | bytes 524320 | tf_op jit(solution)/shard_map/all_to_all | solution.py:99
  168.0 10.4 %all_to_all.94 = f32[16,1,3072]{2,1,0:T(1,128)S(1)} all-to-all(f32[16,1,3072]{2,1,0:T(1,128)S(1)} %bitcast.212), channel_id=1, replica_groups=mesh['gx'=16,'gy'=32] {'gx'}, dimensions={0} | all-to-all | bytes 393216 | tf_op jit(solution)/shard_map/all_to_all | solution.py:99
  179.1 3.9 %all-to-all-start.8 = ((f32[32,1,1024]{2,1,0:T(1,128)}), f32[32,1,1024]{2,1,0:T(1,128)S(1)}, u32[]{:S(2)}, u32[]{:S(2)}) async-start(f32[32,1,1024]{2,1,0:T(1,128)} %bitcast.68), calls=%async_computation.8 | async-start | bytes 262144 | tf_op jit(solution)/shard_map/all_to_all | solution.py:99
  184.5 13.4 %all-to-all-done.8 = f32[32,1,1024]{2,1,0:T(1,128)S(1)} async-done(((f32[32,1,1024]{2,1,0:T(1,128)}), f32[32,1,1024]{2,1,0:T(1,128)S(1)}, u32[]{:S(2)}, u32[]{:S(2)}) %all-to-all-start.8) | async-done | bytes 131104 | tf_op jit(solution)/shard_map/all_to_all | solution.py:99
  199.0 5.8 %all-to-all-start.9 = ((f32[32,1,256]{2,1,0:T(1,128)}), f32[32,1,256]{2,1,0:T(1,128)S(1)}, u32[]{:S(2)}, u32[]{:S(2)}) async-start(f32[32,1,256]{2,1,0:T(1,128)} %bitcast.71), calls=%async_computation.9 | async-start | bytes 65536 | tf_op jit(solution)/shard_map/all_to_all | solution.py:99
  205.4 13.1 %all-to-all-done.9 = f32[32,1,256]{2,1,0:T(1,128)S(1)} async-done(((f32[32,1,256]{2,1,0:T(1,128)}), f32[32,1,256]{2,1,0:T(1,128)S(1)}, u32[]{:S(2)}, u32[]{:S(2)}) %all-to-all-start.9) | async-done | bytes 32800 | tf_op jit(solution)/shard_map/all_to_all | solution.py:99
  (163 shorter events, 22.5 us)
Async XLA Ops:
  0.6 134.8 %copy-start = (f32[32,32]{1,0:T(8,128)S(1)}, f32[32,32]{1,0:T(8,128)}, u32[]{:S(2)}) copy-start(f32[32,32]{1,0:T(8,128)} %param.23) | copy-start | bytes 12292
  2.5 10.7 %collective-permute-start = (f32[3,2,8,256]{3,1,2,0:T(2,128)S(1)}, f32[3,2,8,256]{3,1,2,0:T(2,128)S(1)}, u32[]{:S(2)}, u32[]{:S(2)}) collective-permute-start(f32[3,2,8,256]{3,1,2,0:T(2,128)S(1)} %get-tuple-element.67), channel_id=1, source_target_pairs={{0,32},{32,64},{64,96},{96,128},{128,160},{160,192},{192,224},{224... | collective-permute-start | bytes 147464 | tf_op jit(solution)/shard_map/ppermute | solution.py:91
  7.1 7.0 %collective-permute-start.1 = (f32[3,2,8,256]{3,1,2,0:T(2,128)S(1)}, f32[3,2,8,256]{3,1,2,0:T(2,128)S(1)}, u32[]{:S(2)}, u32[]{:S(2)}) collective-permute-start(f32[3,2,8,256]{3,1,2,0:T(2,128)S(1)} %get-tuple-element.68), channel_id=1, source_target_pairs={{32,0},{64,32},{96,64},{128,96},{160,128},{192,160},{224,192},{256... | collective-permute-start | bytes 147464 | tf_op jit(solution)/shard_map/ppermute | solution.py:92
  14.1 14.1 %collective-permute-start.2 = (f32[3,12,2,256]{3,1,2,0:T(8,128)S(1)}, f32[3,12,2,256]{3,1,2,0:T(8,128)S(1)}, u32[]{:S(2)}, u32[]{:S(2)}) collective-permute-start(f32[3,12,2,256]{3,1,2,0:T(8,128)S(1)} %get-tuple-element.47), channel_id=1, source_target_pairs={{0,1},{1,2},{2,3},{3,4},{4,5},{5,6},{6,7},{7,8},{8,9},{9,10},{10,1... | collective-permute-start | bytes 221192 | tf_op jit(solution)/shard_map/ppermute | solution.py:91
  17.2 12.5 %collective-permute-start.3 = (f32[3,12,2,256]{3,1,2,0:T(8,128)S(1)}, f32[3,12,2,256]{3,1,2,0:T(8,128)S(1)}, u32[]{:S(2)}, u32[]{:S(2)}) collective-permute-start(f32[3,12,2,256]{3,1,2,0:T(8,128)S(1)} %get-tuple-element.48), channel_id=1, source_target_pairs={{1,0},{2,1},{3,2},{4,3},{5,4},{6,5},{7,6},{8,7},{9,8},{10,9},{11,1... | collective-permute-start | bytes 221192 | tf_op jit(solution)/shard_map/ppermute | solution.py:92
  30.7 0.9 copy-start.2
  31.1 0.9 copy-start.4
  31.1 1.1 copy-start.6
  31.8 8.4 %copy-start.1 = (f32[2,2,1,32,1024]{4,3,2,1,0:T(8,128)S(1)}, f32[2,2,1,32,1024]{4,3,2,1,0:T(8,128)}, u32[]{:S(2)}) copy-start(f32[2,2,1,32,1024]{4,3,2,1,0:T(8,128)} %param.22) | copy-start | bytes 1572868
  33.7 27.6 %copy-start.13 = (f32[32,2]{0,1:T(2,128)S(1)}, f32[32,2]{0,1:T(2,128)}, u32[]{:S(2)}) copy-start(f32[32,2]{0,1:T(2,128)} %param.21) | copy-start | bytes 772
  34.5 11.9 %all-to-all-start = ((f32[16,1,2048]{2,1,0:T(1,128)}), f32[16,1,2048]{2,1,0:T(1,128)S(1)}, u32[]{:S(2)}, u32[]{:S(2)}) async-start(f32[16,1,2048]{2,1,0:T(1,128)} %bitcast.20), calls=%async_computation | async-start | bytes 262144 | tf_op jit(solution)/shard_map/all_to_all | solution.py:99
  41.0 53.1 %copy-start.5 = (f32[256,32]{1,0:T(8,128)S(1)}, f32[256,32]{1,0:T(8,128)}, u32[]{:S(2)}) copy-start(f32[256,32]{1,0:T(8,128)} %constant.192) | copy-start | bytes 98308
  46.5 47.8 %copy-start.7 = (f32[256,32]{1,0:T(8,128)S(1)}, f32[256,32]{1,0:T(8,128)}, u32[]{:S(2)}) copy-start(f32[256,32]{1,0:T(8,128)} %constant.193) | copy-start | bytes 98308
  48.4 26.7 %all-to-all-start.1 = ((f32[32,1,256]{2,1,0:T(1,128)}), f32[32,1,256]{2,1,0:T(1,128)S(1)}, u32[]{:S(2)}, u32[]{:S(2)}) async-start(f32[32,1,256]{2,1,0:T(1,128)} %bitcast.22), calls=%async_computation.1 | async-start | bytes 65536 | tf_op jit(solution)/shard_map/all_to_all | solution.py:99
  75.9 53.0 %copy-start.11 = (f32[128,32]{1,0:T(8,128)S(1)}, f32[128,32]{1,0:T(8,128)}, u32[]{:S(2)}) copy-start(f32[128,32]{1,0:T(8,128)} %constant.194) | copy-start | bytes 49156
  94.3 35.2 %copy-start.9 = (f32[128,32]{1,0:T(8,128)S(1)}, f32[128,32]{1,0:T(8,128)}, u32[]{:S(2)}) copy-start(f32[128,32]{1,0:T(8,128)} %constant.195) | copy-start | bytes 49156
  95.4 19.3 %all-to-all-start.3 = ((f32[32,1,1024]{2,1,0:T(1,128)}), f32[32,1,1024]{2,1,0:T(1,128)}, u32[]{:S(2)}, u32[]{:S(2)}) async-start(f32[32,1,1024]{2,1,0:T(1,128)} %bitcast.32), calls=%async_computation.3 | async-start | bytes 262144 | tf_op jit(solution)/shard_map/all_to_all | solution.py:99
  114.8 13.4 %all-to-all-start.4 = ((f32[16,1,2048]{2,1,0:T(1,128)}), f32[16,1,2048]{2,1,0:T(1,128)S(1)}, u32[]{:S(2)}, u32[]{:S(2)}) async-start(f32[16,1,2048]{2,1,0:T(1,128)} %bitcast.33), calls=%async_computation.4 | async-start | bytes 262144 | tf_op jit(solution)/shard_map/all_to_all | solution.py:99
  130.1 5.8 %copy-start.10 = (f32[8,8,256]{2,1,0:T(8,128)S(1)}, f32[8,8,256]{2,1,0:T(8,128)}, u32[]{:S(2)}) copy-start(f32[8,8,256]{2,1,0:T(8,128)} %param.26) | copy-start | bytes 196612
  130.2 5.8 %copy-start.14 = (f32[32]{0:T(128)S(1)}, f32[32]{0:T(128)}, u32[]{:S(2)}) copy-start(f32[32]{0:T(128)} %param.25) | copy-start | bytes 388
  130.2 6.0 %copy-start.15 = (f32[32]{0:T(128)S(1)}, f32[32]{0:T(128)}, u32[]{:S(2)}) copy-start(f32[32]{0:T(128)} %param.24) | copy-start | bytes 388
  130.2 15.0 %copy-start.16 = (f32[2,256,128,1]{2,1,0,3:T(8,128)S(1)}, f32[2,256,128,1]{2,1,0,3:T(8,128)}, u32[]{:S(2)}) copy-start(f32[2,256,128,1]{2,1,0,3:T(8,128)} %constant.198) | copy-start | bytes 786436
  131.4 13.8 %all-to-all-start.5 = ((f32[16,1,8192]{2,1,0:T(1,128)}), f32[16,1,8192]{2,1,0:T(1,128)S(1)}, u32[]{:S(2)}, u32[]{:S(2)}) async-start(f32[16,1,8192]{2,1,0:T(1,128)} %bitcast.40), calls=%async_computation.5 | async-start | bytes 1048576 | tf_op jit(solution)/shard_map/all_to_all | solution.py:99
  150.1 1.0 copy-start.3
  150.3 16.9 %copy-start.12 = (f32[64,128]{1,0:T(8,128)S(1)}, f32[64,128]{1,0:T(8,128)}, u32[]{:S(2)}) copy-start(f32[64,128]{1,0:T(8,128)} %constant.179.clone) | copy-start | bytes 98308
  152.9 14.4 %all-to-all-start.6 = ((f32[16,1,8192]{2,1,0:T(1,128)}), f32[16,1,8192]{2,1,0:T(1,128)S(1)}, u32[]{:S(2)}, u32[]{:S(2)}) async-start(f32[16,1,8192]{2,1,0:T(1,128)} %bitcast.54), calls=%async_computation.6 | async-start | bytes 1048576 | tf_op jit(solution)/shard_map/all_to_all | solution.py:99
  167.6 30.4 %copy-start.8 = (f32[64,256]{1,0:T(8,128)S(1)}, f32[64,256]{1,0:T(8,128)}, u32[]{:S(2)}) copy-start(f32[64,256]{1,0:T(8,128)} %constant.180.clone) | copy-start | bytes 196612
  179.1 18.8 %all-to-all-start.8 = ((f32[32,1,1024]{2,1,0:T(1,128)}), f32[32,1,1024]{2,1,0:T(1,128)S(1)}, u32[]{:S(2)}, u32[]{:S(2)}) async-start(f32[32,1,1024]{2,1,0:T(1,128)} %bitcast.68), calls=%async_computation.8 | async-start | bytes 262144 | tf_op jit(solution)/shard_map/all_to_all | solution.py:99
  199.0 19.5 %all-to-all-start.9 = ((f32[32,1,256]{2,1,0:T(1,128)}), f32[32,1,256]{2,1,0:T(1,128)S(1)}, u32[]{:S(2)}, u32[]{:S(2)}) async-start(f32[32,1,256]{2,1,0:T(1,128)} %bitcast.71), calls=%async_computation.9 | async-start | bytes 65536 | tf_op jit(solution)/shard_map/all_to_all | solution.py:99

commit v2 on v1

v2 whole, which is shorter than its diff:
```python
import math

import numpy as np

import jax
import jax.numpy as jnp
from jax import lax
from jax.experimental import pallas as pl
from jax.experimental.pallas import tpu as pltpu
from jax.sharding import PartitionSpec as P

TIME_STEP = 0.05
COUPLING = 2.0
SOLID_DIFF = 0.05
LIQUID_DIFF = 1.0
PARTITION = 0.15
TRAP_RATE = 4.0
SOLUTE_MEAN = 0.5
GELU_K = math.sqrt(2.0 / math.pi)
GELU_C = 0.044715
F32 = jnp.float32
MESH = pl.DeviceIdType.MESH


def signed(count):
    index = np.arange(count)
    return np.where(index < count // 2, index, index - count)


def trig(freqs, places, length, factor=1.0):
    angle = 2.0 * np.pi * ((freqs[:, None] * places[None, :]) % length) / length
    return np.cos(angle) * factor, np.sin(angle) * factor


def z_tables(modes, depth):
    cos, sin = trig(np.arange(modes), np.arange(depth), depth)
    lanes = 2 * modes
    weight = np.where(np.arange(modes) == 0, 1.0, 2.0) / depth
    both = np.stack([cos, -sin])

    def blocks(one):
        full = np.zeros((2 * depth, 2 * lanes))
        full[:depth, :lanes] = one
        full[depth:, lanes:] = one
        return full

    plain = both.reshape(lanes, depth).T
    heavy = (both * weight[None, :, None]).reshape(lanes, depth).T
    return blocks(plain), blocks(heavy), blocks(heavy).T


def tables(gx, gy, cx, cy, depth, kx, ky, kz):
    nx, ny = gx * cx, gy * cy
    own = kx // gx
    zf, zg, zi = z_tables(kz, depth)
    cosx, sinx = trig(signed(kx), np.arange(nx), nx)
    cosy, siny = trig(signed(ky), np.arange(ny), ny)
    tx = np.concatenate([cosx, sinx]).reshape(2 * kx, gx, cx).transpose(1, 2, 0)
    ty = np.zeros((gy, own, cy, 2, ky, own))
    both = np.stack([cosy, siny]).reshape(2, ky, gy, cy).transpose(2, 3, 0, 1)
    for k in range(own):
        ty[:, k, :, :, :, k] = both
    ty = ty.reshape(gy, own * cy, 2 * ky * own)
    tyi = np.concatenate([cosy, -siny]).T / ny
    txi = np.concatenate([cosx, -sinx]).T / nx
    txf = np.stack([cosx, sinx]).reshape(2, gx, own, nx).transpose(0, 2, 1, 3).reshape(2 * kx, nx) / nx
    tyf = np.concatenate([cosy, siny]) / ny
    return [np.asarray(t, np.float32) for t in (zf, zg, zi, tx, ty, tyi, txi, txf, tyf)]


def dot(a, b, dims=((1,), (0,))):
    return lax.dot_general(a, b, (dims, ((), ())), precision=lax.Precision.HIGHEST, preferred_element_type=F32)


def iota(shape, dim):
    return lax.broadcasted_iota(jnp.int32, shape, dim)


def rot(v):
    imag = (iota(v.shape, 1) // 32) % 2 == 1
    return jnp.where(imag, -pltpu.roll(v, 32, 1), pltpu.roll(v, 96, 1))


def diffusivity(p):
    return SOLID_DIFF + (LIQUID_DIFF - SOLID_DIFF) * 0.5 * (1.0 - jnp.tanh(p))


def around(ref, x):
    centre = ref[x]
    rows, depth = centre.shape
    return centre, [
        ref[x + 1],
        ref[x - 1],
        pltpu.roll(centre, rows - 1, 0),
        pltpu.roll(centre, 1, 0),
        pltpu.roll(centre, depth - 1, 1),
        pltpu.roll(centre, 1, 1),
    ]


def advance(p_ref, c_ref, d_ref, undercool, x):
    p, p_nb = around(p_ref, x)
    c, c_nb = around(c_ref, x)
    d, d_nb = around(d_ref, x)
    total = p_nb[0]
    for one in p_nb[1:]:
        total = total + one
    squares = 1.0 - p * p
    rate = total - 6.0 * p + p - p * p * p + COUPLING * squares * squares * (undercool - c)
    div = 0.0
    for dn, cn in zip(d_nb, c_nb):
        div = div + 0.5 * (d + dn) * (cn - c)
    speed = TRAP_RATE * jnp.abs(rate)
    keff = (PARTITION + speed) / (1.0 + speed)
    return p + TIME_STEP * rate, c + TIME_STEP * (div + 0.5 * (1.0 - keff) * c * rate)


def kernel(
    dims, phase, solute, undercool, cotangent, weight, lift, local, bias, proj,
    zf, zg, zi, tx, ty, tyi, txi, txf, tyf,
    phase_out, solute_out, predicted_out, spectral_out, local_out, proj_out,
    yhi, ylo, from_ylo, from_yhi, from_corner, from_xlo, from_xhi,
    pad_p, pad_c, pad_d, pad_u, mid_p, mid_c, mid_d, flat, cells, cot, total, coef, lifted, blend, source, field, sums,
    send1, recv1, send2, recv2, send3, recv3, send4, recv4, recv5, send6, recv6, send7, recv7,
    send8, recv8, recv9, send10, recv10, send11, recv11, modes,
    halo_send, halo_recv, send_sem, recv_sem, recv6_sem,
):
    gx, gy, group = dims
    ix, iy = lax.axis_index("gx"), lax.axis_index("gy")
    east, west = lax.rem(ix + 1, gx), lax.rem(ix + gx - 1, gx)
    north, south = lax.rem(iy + 1, gy), lax.rem(iy + gy - 1, gy)
    width = lift.shape[0]
    pairs = width // 2
    kx, ky = 2 * gx, gy
    square = width * width
    barrier = pltpu.get_barrier_semaphore()

    def greet(axis, mine, count):
        def one(j, carry):
            pl.semaphore_signal(barrier, inc=1, device_id={axis: lax.rem(mine + j, count)}, device_id_type=MESH)
            return carry

        lax.fori_loop(1, count, one, 0)

    for a in (east, west):
        for b in (north, south):
            pl.semaphore_signal(barrier, inc=1, device_id={"gx": a, "gy": b}, device_id_type=MESH)
    greet("gx", ix, gx)
    greet("gy", iy, gy)

    row = iota((8, 8, phase.shape[2]), 1)
    p, c, u = phase[...], solute[...], undercool[...]
    yhi[...] = jnp.where(row >= 6, p, jnp.where(row >= 4, pltpu.roll(c, 6, 1), pltpu.roll(u, 4, 1)))
    ylo[...] = jnp.where(row < 2, p, jnp.where(row < 4, pltpu.roll(c, 2, 1), pltpu.roll(u, 4, 1)))
    pad_p[2:10, 8:16, :] = p
    pad_c[2:10, 8:16, :] = c
    pad_u[1:9, 8:16, :] = u

    lane = iota((width, square), 1)
    inner = lane % width == iota((width, square), 0)
    for k in range(2):
        spread = jnp.where(inner, jnp.broadcast_to(lift[:, k : k + 1], (width, square)), 0.0)
        lifted[k : k + 1, :] = jnp.sum(spread, axis=0, keepdims=True)
        column = jnp.broadcast_to(lift[:, k : k + 1], (width, 128))
        coef[k * width : (k + 1) * width] = dot(local[...], column).reshape(width, 1, 128)
    eye = iota((width, width), 0) == iota((width, width), 1)
    for k, vector in ((2, bias), (3, proj)):
        diagonal = jnp.where(eye, jnp.broadcast_to(vector[...], (width, width)), 0.0)
        coef[k * width : (k + 1) * width] = dot(diagonal, jnp.ones((width, 128), F32)).reshape(width, 1, 128)
    outer = jnp.where(lane // width == iota((width, square), 0), 1.0, 0.0)
    src, dst = iota((128, 128), 0), iota((128, 128), 1)
    for k in range(2):
        both = dot(outer, weight[...] * lifted[k : k + 1, :], ((1,), (1,)))
        for part in range(2):
            for x in range(2):
                value = 0.0
                for par in range(2):
                    pick = (src % 32 == dst % 32) & (src // 32 == part * 2 + x) & (dst // 64 == par)
                    value = value + dot(both[par * pairs : (par + 1) * pairs], jnp.where(pick, 1.0, 0.0))
                blend[2 * k + part, pl.ds(x, pairs, stride=2), :] = value
    sums[...] = jnp.zeros_like(sums)
    total[...] = jnp.zeros_like(total)
    depth = phase.shape[2]
    for x in range(8):
        for h in range(2):
            flat[h, 8 * x : 8 * x + 8, :] = cotangent[x, :, 128 * h : 128 * h + 128]
    for y in range(8):
        for h in range(2):
            cot[8 * y : 8 * y + 8, 128 * h : 128 * h + 128] = flat[h, pl.ds(y, 8, stride=8), :]

    pl.semaphore_wait(barrier, 4 + gx - 1 + gy - 1)

    def push(source_ref, target_ref, slot, where):
        copy = pltpu.make_async_remote_copy(
            src_ref=source_ref,
            dst_ref=target_ref,
            send_sem=halo_send.at[slot],
            recv_sem=halo_recv.at[slot],
            device_id=where,
            device_id_type=MESH,
        )
        copy.start()
        return copy

    copies = [
        push(yhi, from_ylo, 0, {"gy": north}),
        push(ylo, from_yhi, 1, {"gy": south}),
        push(yhi.at[7], from_corner.at[0], 2, {"gx": east, "gy": north}),
        push(yhi.at[0], from_corner.at[1], 3, {"gx": west, "gy": north}),
        push(ylo.at[7], from_corner.at[2], 4, {"gx": east, "gy": south}),
        push(ylo.at[0], from_corner.at[3], 5, {"gx": west, "gy": south}),
        push(phase.at[6:8], from_xlo.at[0:2], 6, {"gx": east}),
        push(solute.at[6:8], from_xlo.at[2:4], 7, {"gx": east}),
        push(undercool.at[7:8], from_xlo.at[4:5], 8, {"gx": east}),
        push(phase.at[0:2], from_xhi.at[0:2], 9, {"gx": west}),
        push(solute.at[0:2], from_xhi.at[2:4], 10, {"gx": west}),
        push(undercool.at[0:1], from_xhi.at[4:5], 11, {"gx": west}),
    ]
    for copy in copies:
        copy.wait_recv()

    def lay(rows, low, planes):
        at = slice(0, 8) if low else slice(16, 24)
        turn = 1 if low else -1
        pad_p[planes, at, :] = rows
        pad_c[planes, at, :] = pltpu.roll(rows, (2 * turn) % 8, 1)
        pad_u[slice(planes.start - 1, planes.stop - 1), at, :] = pltpu.roll(rows, 4, 1)

    lay(from_ylo[...], True, slice(2, 10))
    lay(from_yhi[...], False, slice(2, 10))
    lay(from_corner[0:1], True, slice(1, 2))
    lay(from_corner[1:2], True, slice(10, 11))
    lay(from_corner[2:3], False, slice(1, 2))
    lay(from_corner[3:4], False, slice(10, 11))
    pad_p[0:2, 8:16, :] = from_xlo[0:2]
    pad_c[0:2, 8:16, :] = from_xlo[2:4]
    pad_u[0:1, 8:16, :] = from_xlo[4:5]
    pad_p[10:12, 8:16, :] = from_xhi[0:2]
    pad_c[10:12, 8:16, :] = from_xhi[2:4]
    pad_u[9:10, 8:16, :] = from_xhi[4:5]

    def first_diff(x, carry):
        pad_d[x] = diffusivity(pad_p[x])
        return carry

    def first(x, carry):
        new_p, new_c = advance(pad_p, pad_c, pad_d, pad_u[x], x + 1)
        mid_p[x] = new_p
        mid_c[x] = new_c
        mid_d[x] = diffusivity(new_p)
        return carry

    def second(x, carry):
        new_p, new_c = advance(mid_p, mid_c, mid_d, pad_u[x + 1], x + 1)
        new_p, new_c = new_p[8:16], new_c[8:16]
        phase_out[x] = new_p
        solute_out[x] = new_c
        at = pl.multiple_of(8 * x, 8)
        for h in range(2):
            flat[h, pl.ds(at, 8), :] = new_p[:, 128 * h : 128 * h + 128]
            flat[2 + h, pl.ds(at, 8), :] = new_c[:, 128 * h : 128 * h + 128] - SOLUTE_MEAN
        return carry

    lax.fori_loop(0, 12, first_diff, 0)
    lax.fori_loop(0, 10, first, 0)
    lax.fori_loop(0, 8, second, 0)
    for y in range(8):
        for h in range(4):
            cells[8 * y : 8 * y + 8, 128 * h : 128 * h + 128] = flat[h, pl.ds(y, 8, stride=8), :]

    def exchange(axis, phase_id, sends, receives):
        mine, count = (ix, gx) if axis == "gx" else (iy, gy)
        pltpu.make_async_copy(sends(mine), receives(mine), recv_sem.at[phase_id]).start()

        def one(j, carry):
            peer = lax.rem(mine + j, count)
            pltpu.make_async_remote_copy(
                src_ref=sends(peer),
                dst_ref=receives(mine),
                send_sem=send_sem.at[phase_id],
                recv_sem=recv_sem.at[phase_id],
                device_id={axis: peer},
                device_id_type=MESH,
            ).start()
            return carry

        lax.fori_loop(1, count, one, 0)

    def arrived(phase_id, whole):
        pltpu.make_async_copy(whole, whole, recv_sem.at[phase_id]).wait()

    along = dot(cells[...], zf[...])
    lines = jnp.concatenate([along[8 * y : 8 * y + 8] for y in range(8)], axis=1)
    wave = dot(tx[ix].T, lines)
    for y in range(8):
        at = slice(128 * y, 128 * y + 128)
        send1[pl.ds(y, kx, stride=8), :] = wave[:kx, at] + rot(wave[kx:, at])
    exchange("gx", 1, lambda q: send1.at[pl.ds(pl.multiple_of(16 * q, 16), 16)], lambda q: recv1.at[q])
    arrived(1, recv1)
    got = recv1[0]
    for q in range(1, gx):
        got = got + recv1[q]
    wave = dot(ty[iy].T, got)
    wave = wave[: 2 * ky] + rot(wave[2 * ky :])
    send2[...] = wave.reshape(2 * ky, 1, 128)
    exchange("gy", 2, lambda q: send2.at[pl.ds(2 * q, 2)], lambda q: recv2.at[pl.ds(2 * q, 2)])
    arrived(2, recv2)
    got = recv2[...].reshape(gy, 2, 128).sum(0)

    even = iota((gy, 128), 0) % 2 == 0
    spread = jnp.where(even, jnp.broadcast_to(got[0:1], (gy, 128)), jnp.broadcast_to(got[1:2], (gy, 128)))
    turned = pltpu.roll(spread, 64, 1)
    low = iota((gy, 128), 1) < 64
    value = 0.0
    for k in range(2):
        one = jnp.where(low, spread, turned) if k == 0 else jnp.where(low, turned, spread)
        value = value + blend[2 * k] * one - blend[2 * k + 1] * rot(one)
    send3[...] = value.reshape(gy, 1, 128)
    exchange("gy", 3, lambda q: send3.at[pl.ds(q, 1)], lambda q: recv3.at[pl.ds(q, 1)])

    for x in range(2):
        diagonal = jnp.where(src == dst, jnp.broadcast_to(got[x : x + 1], (128, 128)), 0.0)
        column = jnp.sum(diagonal, axis=1, keepdims=True)
        source[64 * x : 64 * x + 64, :] = column[:64] * lifted[0:1, :] + column[64:] * lifted[1:2, :]

    arrived(3, recv3)
    got = recv3[...].reshape(ky, 128)
    send4[...] = dot(tyi[...], jnp.concatenate([got, rot(got)], axis=0)).reshape(gy, 8, 128)
    exchange("gy", 4, lambda q: send4.at[q], lambda q: recv4.at[q])
    arrived(4, recv4)
    exchange("gx", 5, lambda q: recv4.at[pl.ds(2 * q, 2)], lambda q: recv5.at[pl.ds(2 * q, 2)])
    arrived(5, recv5)
    lines = []
    for y in range(8):
        got = recv5[:, y, :]
        lines.append(jnp.concatenate([got, rot(got)], axis=0))
    wave = dot(txi[...], jnp.concatenate(lines, axis=1))
    for y in range(8):
        send6[:, y] = wave[:, 128 * y : 128 * y + 128].reshape(gx, 8, 128)

    pltpu.make_async_copy(send6.at[ix], recv6.at[ix], recv6_sem.at[ix]).start()

    def give(j, carry):
        peer = lax.rem(ix + j, gx)
        pltpu.make_async_remote_copy(
            src_ref=send6.at[peer],
            dst_ref=recv6.at[ix],
            send_sem=send_sem.at[6],
            recv_sem=recv6_sem.at[ix],
            device_id={"gx": peer},
            device_id_type=MESH,
        ).start()
        return carry

    lax.fori_loop(1, gx, give, 0)

    def wide(o):
        one = coef[o]
        return jnp.concatenate([one, one], axis=1)

    def step(j, carry):
        owners = [lax.rem(ix + gx - (j * group + t), gx) for t in range(group)]
        for owner in owners:
            pltpu.make_async_copy(recv6.at[owner], recv6.at[owner], recv6_sem.at[owner]).wait()
        got = jnp.concatenate([recv6[owner].reshape(64, 128) for owner in owners], axis=0)
        field[...] = dot(got, zi[...])
        for t, owner in enumerate(owners):
            factors = [[wide(k * width + par * pairs + owner) for k in range(4)] for par in range(2)]

            def block(r, acc):
                at = pl.multiple_of(8 * r, 8)
                here = pl.ds(pl.multiple_of(64 * t + 8 * r, 8), 8)
                p, c, w = cells[pl.ds(at, 8), :depth], cells[pl.ds(at, 8), depth:], cot[pl.ds(at, 8), :]
                acc = list(acc)
                out = total[pl.ds(at, 8), :]
                for par in range(2):
                    m0, m1, b, q = factors[par]
                    side = slice(par * depth, (par + 1) * depth)
                    pre = field[here, side] + m0 * p + m1 * c + b
                    power = pre * pre
                    tanh = jnp.tanh(GELU_K * (pre + GELU_C * (power * pre)))
                    half = 0.5 * (1.0 + tanh)
                    act = pre * half
                    slope = half + (0.5 * GELU_K) * pre * (1.0 - tanh * tanh) * (1.0 + (3.0 * GELU_C) * power)
                    out = out + q * act
                    grad = q * w * slope
                    field[here, side] = grad
                    acc[3 * par] = acc[3 * par] + grad * p
                    acc[3 * par + 1] = acc[3 * par + 1] + grad * c
                    acc[3 * par + 2] = acc[3 * par + 2] + act * w
                total[pl.ds(at, 8), :] = out
                return tuple(acc)

            zero = jnp.zeros((8, depth), F32)
            acc = lax.fori_loop(0, 8, block, (zero,) * 6)
            for par in range(2):
                for k in range(3):
                    one = jnp.sum(acc[3 * par + k], axis=0, keepdims=True)
                    sums[k * width + par * pairs + owner] = one[:, :128] + one[:, 128:]
        wave = dot(field[...], zg[...])
        for t, owner in enumerate(owners):
            send7[owner] = wave[64 * t : 64 * t + 64].reshape(8, 8, 128)

            @pl.when(owner == ix)
            def _():
                pltpu.make_async_copy(send7.at[owner], recv7.at[ix], recv_sem.at[7]).start()

            @pl.when(owner != ix)
            def _():
                pltpu.make_async_remote_copy(
                    src_ref=send7.at[owner],
                    dst_ref=recv7.at[ix],
                    send_sem=send_sem.at[7],
                    recv_sem=recv_sem.at[7],
                    device_id={"gx": owner},
                    device_id_type=MESH,
                ).start()

        return carry

    lax.fori_loop(0, gx // group, step, 0)
    for h in range(2):
        flat[h] = total[:, 128 * h : 128 * h + 128]
    for x in range(8):
        for h in range(2):
            predicted_out[x, :, 128 * h : 128 * h + 128] = flat[h, pl.ds(x, 8, stride=8), :]
    added = dot(jnp.ones((8, 128), F32), sums[...].reshape(128, 128), ((1,), (1,)))
    for q in range(gx):
        send8[24 * q + 16 : 24 * q + 24, :] = added

    arrived(7, recv7)
    lines = [recv7[:, y].reshape(8 * gx, 128) for y in range(8)]
    wave = dot(txf[...], jnp.concatenate(lines, axis=1))
    for y in range(8):
        at = slice(128 * y, 128 * y + 128)
        one = wave[:kx, at] + rot(wave[kx:, at])
        for k in range(2):
            send8[pl.ds(8 * k + y, gx, stride=24), :] = one[k * gx : (k + 1) * gx]
    exchange("gx", 8, lambda q: send8.at[pl.ds(pl.multiple_of(24 * q, 8), 24)], lambda q: recv8.at[pl.ds(pl.multiple_of(24 * q, 8), 24)])
    arrived(8, recv8)

    def part(q):
        return recv8.at[pl.ds(pl.multiple_of(24 * (q // 2) + 8 * (q % 2), 8), 8)]

    exchange("gy", 9, part, lambda q: recv9.at[q])
    added = recv8[pl.ds(16, gx, stride=24), :].sum(0, keepdims=True)
    send11[...] = added.reshape(1, 1, 128)
    exchange("gy", 11, lambda q: send11, lambda q: recv11.at[pl.ds(q, 1)])
    arrived(9, recv9)
    wave = dot(tyf[...], recv9[...].reshape(8 * gy, 128))
    wave = wave[:ky] + rot(wave[ky:])
    send10[...] = wave.reshape(ky, 1, 128)
    exchange("gy", 10, lambda q: send10.at[pl.ds(q, 1)], lambda q: recv10.at[pl.ds(q, 1)])

    scale = 1.0 / math.sqrt(8 * gx * 8 * gy * depth)
    arrived(11, recv11)
    added = recv11[...].reshape(gy, 128).sum(0, keepdims=True) * scale
    place = iota((width, 128), 1) - iota((width, 128), 0)
    value = 0.0
    for k in range(2):
        picked = jnp.where(place == k * width, jnp.broadcast_to(added, (width, 128)), 0.0)
        value = value + jnp.sum(picked, axis=1, keepdims=True) * lifted[k : k + 1, :width]
    local_out[...] = value
    pick = iota((128, width), 0) - iota((128, width), 1) == 2 * width
    proj_out[...] = dot(jnp.broadcast_to(added, (8, 128)), jnp.where(pick, 1.0, 0.0))[0:1]

    arrived(10, recv10)
    modes[...] = recv10[...].reshape(gy, 128)
    for x in range(2):
        got = modes[pl.ds(x, pairs, stride=2), :]
        got = jnp.concatenate([got, pltpu.roll(got, 64, 1)], axis=0).T[:64]
        grad = dot(got, outer)
        re, im = grad[:32], grad[32:]
        base = 64 * x
        s_re, s_im = source[base : base + 32, :], source[base + 32 : base + 64, :]
        spectral_out[0, x, 0] = re * s_re + im * s_im
        spectral_out[1, x, 0] = im * s_re - re * s_im

    for copy in copies:
        copy.wait_send()
    for phase_id, whole in (
        (1, recv1.at[1:gx]),
        (2, send2.at[2 : 2 * gy]),
        (3, send3.at[1:gy]),
        (4, send4.at[1:gy]),
        (5, recv4.at[2 : 2 * gx]),
        (6, send6.at[1:gx]),
        (7, send7.at[1:gx]),
        (8, send8.at[24 : 24 * gx]),
        (9, recv9.at[1:gy]),
        (10, send10.at[1:gy]),
        (11, recv11.at[1:gy]),
    ):
        pltpu.make_async_copy(whole, whole, send_sem.at[phase_id]).wait()


def per_device(phase, solute, undercool, lift, weight, local, bias, proj, cotangent):
    gx, gy = lax.axis_size("gx"), lax.axis_size("gy")
    cx, cy, depth = phase.shape
    own_kx, own_ky, kz = weight.shape[1:4]
    width = lift.shape[0]
    square = width * width
    assert width == 2 * gx and gy == 2 * gx and (cx, cy, own_kx, own_ky, kz) == (8, 8, 2, 1, 32)
    consts = tables(gx, gy, cx, cy, depth, gx * own_kx, gy * own_ky, kz)
    group = min(4, gx)
    vmem = pl.BlockSpec(memory_space=pltpu.VMEM)
    buf = lambda *shape: pltpu.VMEM(shape, F32)
    tile = jax.ShapeDtypeStruct((cx, cy, depth), F32)
    outs = (
        tile, tile, tile,
        jax.ShapeDtypeStruct(weight.shape, F32),
        jax.ShapeDtypeStruct((width, width), F32),
        jax.ShapeDtypeStruct((1, width), F32),
    )
    scratch = [
        buf(8, 8, depth), buf(8, 8, depth), buf(8, 8, depth), buf(8, 8, depth), buf(4, 8, depth), buf(5, 8, depth), buf(5, 8, depth),
        buf(12, 24, depth), buf(12, 24, depth), buf(12, 24, depth), buf(10, 24, depth),
        buf(10, 24, depth), buf(10, 24, depth), buf(10, 24, depth),
        buf(4, 64, 128), buf(64, 2 * depth), buf(64, depth), buf(64, depth),
        buf(4 * width, 1, 128), buf(2, square), buf(4, gy, 128), buf(128, square), buf(64 * group, 2 * depth), buf(128, 1, 128),
        buf(16 * gx, 128), buf(gx, 16, 128), buf(2 * gy, 1, 128), buf(2 * gy, 1, 128), buf(gy, 1, 128), buf(gy, 1, 128),
        buf(gy, 8, 128), buf(gy, 8, 128), buf(2 * gx, 8, 128), buf(gx, 8, 8, 128), buf(gx, 8, 8, 128),
        buf(gx, 8, 8, 128), buf(gx, 8, 8, 128), buf(24 * gx, 128), buf(24 * gx, 128), buf(gy, 8, 128),
        buf(gy, 1, 128), buf(gy, 1, 128), buf(1, 1, 128), buf(gy, 1, 128), buf(gy, 128),
        pltpu.SemaphoreType.DMA((12,)), pltpu.SemaphoreType.DMA((12,)),
        pltpu.SemaphoreType.DMA((12,)), pltpu.SemaphoreType.DMA((12,)), pltpu.SemaphoreType.DMA((gx,)),
    ]
    args = [phase, solute, undercool, cotangent, weight.reshape(128, square), lift, local, bias.reshape(1, -1), proj.reshape(1, -1)]
    args += [jnp.asarray(t) for t in consts]
    got = pl.pallas_call(
        lambda *refs: kernel((gx, gy, group), *refs),
        out_shape=outs,
        in_specs=[vmem] * len(args),
        out_specs=(vmem,) * len(outs),
        scratch_shapes=scratch,
        compiler_params=pltpu.CompilerParams(collective_id=0, has_side_effects=True, vmem_limit_bytes=48 * 2**20),
        name="layer",
    )(*args)
    return (*got[:5], got[5].reshape(width))


def solution(mesh):
    tile, modes = P("gx", "gy", None), P(None, "gx", "gy", None, None)
    return jax.shard_map(
        per_device,
        mesh=mesh,
        in_specs=(tile, tile, tile, P(), modes, P(), P(), P(), tile),
        out_specs=(tile, tile, tile, modes, P(), P()),
        check_vma=False,
    )
```

time: 225 us -> 131 us (0.58)
  Pallas kernels: 0 us -> 113 us
  waiting for transfers between devices: 83 us -> 0 us
  starting transfers between devices: 73.4 us -> 0 us
  blocking collectives: 28.2 us -> 0 us
  matrix products: 15 us -> 0 us
  other arithmetic: 4.03 us -> 0 us
    pallas_call x0 -> x1, Pallas kernels: none -> 113 us  [per_device(): pl.pallas_call(lambda *refs: kernel((gx, gy, group), *refs), out_shape=ou...]
    all_to_all x8 -> x0, waiting for transfers between devices: 80.6 us -> none  [swap(): lax.all_to_all(flat, axis, split_axis=0, concat_axis=0, tiled=True)]
    all_to_all x8 -> x0, starting transfers between devices: 48.8 us -> none  [swap(): lax.all_to_all(flat, axis, split_axis=0, concat_axis=0, tiled=True)]
    all_to_all x2 -> x0, blocking collectives: 28.2 us -> none  [swap(): lax.all_to_all(flat, axis, split_axis=0, concat_axis=0, tiled=True)]
    ppermute x4 -> x0, starting transfers between devices: 24.6 us -> none  [the longest x2 16.9 us: extended(): lax.ppermute(head, axis, [((i + 1) % count, i) for i in range(count)])]
    dot_general x16 -> x0, matrix products: 15 us -> none  [the longest x10 7.68 us: mm(): jnp.dot(a, b, precision=lax.Precision.HIGH, preferred_element_type=F32)]
    unnamed x43 -> x41, local copies, waits for them, and re-layouts: 4.16 us -> 16.9 us
    slice x32 -> x0, local copies, waits for them, and re-layouts: 2.92 us -> none  [the longest x10 0.81 us: rot(): jnp.roll(v, -quarter, v.ndim - 1)]
  transfers between devices with their start and end apart: 12 -> 0, of which waited for: 11 -> 0; matrix products, arithmetic and copies ran while one was open for 4% -> 0% of each run, Pallas kernels for 0% -> 0%
where the time goes in v2:
time: 131 us; the launch traced here: 130 us
  Pallas kernels  113 us (86%)
  local copies, waits for them, and re-layouts  16.9 us (13%)
    pallas_call x1, Pallas kernels, per_device(): pl.pallas_call(lambda *refs: kernel((gx, gy, group), *refs), out_shape=ou...  113 us
    unnamed x41, local copies, waits for them, and re-layouts  16.9 us

profile of v2, /device:TPU:1, one launch (start us, length us, event | category | flops | bytes accessed | tf_op | source)
XLA Modules:
  0.0 130.4 jit_solution(11264194836424886109)
XLA Ops:
  0.6 0.0 copy-start.13
  0.6 0.0 copy-start.15
  0.7 0.0 copy-start.16
  0.7 0.8 copy.24.refs_5_
  1.4 0.0 copy-done.13
  1.4 0.0 copy-done.15
  1.4 0.0 copy-done.16
  1.5 0.0 copy-start
  1.5 1.0 copy-done
  2.5 0.0 copy-start.1
  2.5 0.9 copy-done.1
  3.5 0.0 copy-start.2
  3.5 0.9 copy-done.2
  4.4 0.0 copy-start.3
  4.4 0.9 copy-done.3
  5.4 0.9 copy-done.4
  6.3 0.9 copy-done.5
  7.2 0.8 copy-done.6
  8.1 0.8 copy-done.7
  8.9 0.8 copy-done.8
  9.7 0.8 copy-done.9
  10.6 0.8 copy-done.10
  11.4 0.8 copy-done.11
  12.3 0.8 copy-done.12
  13.1 0.7 copy-done.14
  13.8 112.8 %layer.1 = (f32[8,8,256]{2,1,0:T(8,128)S(1)}, f32[8,8,256]{2,1,0:T(8,128)S(1)}, f32[8,8,256]{2,1,0:T(8,128)S(1)}, f32[2,2,1,32,1024]{4,3,2,1,0:T(8,128)S(1)}, f32[32,32]{1,0:T(8,128)S(1)}, /*index=5*/f32[1,32]{1,0:T(1,128)S(1)}) custom-call(f32[8,8,256]{2,1,0:T(8,128)S(1)} %copy-done.6, f32[8,8,256]{2,1,0:T(8,128)S(1)} %copy-done.7, ...), custom_call_target="tpu_custom_call" | custom-call | tf_op jit(solution)/shard_map/layer/pallas_call | solution.py:530
  126.6 0.6 copy.31
  127.3 0.6 copy.32
  127.9 0.6 copy.33
  128.5 0.8 copy.34
  129.3 0.6 copy.35
  129.9 0.5 copy.36
  (10 shorter events, 0.0 us)
Async XLA Ops:
  0.6 0.8 copy-start.13
  0.6 0.8 copy-start.15
  0.7 0.8 copy-start.16
  1.5 1.0 copy-start
  2.5 0.9 copy-start.1
  3.5 0.9 copy-start.2
  4.4 0.9 copy-start.3
  5.4 0.9 copy-start.4
  6.3 0.9 copy-start.5
  7.2 0.8 copy-start.6
  8.0 0.8 copy-start.7
  8.9 0.8 copy-start.8
  9.7 0.8 copy-start.9
  10.6 0.8 copy-start.10
  11.4 0.8 copy-start.11
  12.2 0.8 copy-start.12
  13.1 0.7 copy-start.14

commit v3 on v2

--- a/solution.py
+++ b/solution.py
@@ -65,7 +65,37 @@
     txi = np.concatenate([cosx, -sinx]).T / nx
     txf = np.stack([cosx, sinx]).reshape(2, gx, own, nx).transpose(0, 2, 1, 3).reshape(2 * kx, nx) / nx
     tyf = np.concatenate([cosy, siny]) / ny
-    return [np.asarray(t, np.float32) for t in (zf, zg, zi, tx, ty, tyi, txi, txf, tyf)]
+    right = [in_three(t, 0) for t in (zf, zg, zi)]
+    left = [in_three(t, 1) for t in (tyi, txi, txf, tyf)]
+    return right + [np.asarray(tx, np.float32), np.asarray(ty, np.float32)] + left
+
+
+def in_three(table, axis):
+    table = np.asarray(table, np.float32)
+    high = table.astype(jnp.bfloat16)
+    low = (table - high.astype(np.float32)).astype(jnp.bfloat16)
+    return np.concatenate([high, low, high], axis=axis)
+
+
+def parts(v, axis, order):
+    high = v.astype(jnp.bfloat16)
+    low = (v - high.astype(F32)).astype(jnp.bfloat16)
+    return jnp.concatenate([(high, low)[k] for k in order], axis=axis)
+
+
+def dot_right(v, table):
+    return jnp.dot(parts(v, 1, (0, 0, 1)), table, preferred_element_type=F32)
+
+
+def dot_left(table, v):
+    return jnp.dot(table, parts(v, 0, (0, 0, 1)), preferred_element_type=F32)
+
+
+def dot_pick(v, pick):
+    high = v.astype(jnp.bfloat16)
+    low = (v - high.astype(F32)).astype(jnp.bfloat16)
+    pick = pick.astype(jnp.bfloat16)
+    return jnp.dot(high, pick, preferred_element_type=F32) + jnp.dot(low, pick, preferred_element_type=F32)
 
 
 def dot(a, b, dims=((1,), (0,))):
@@ -116,20 +146,21 @@
 
 
 def kernel(
-    dims, phase, solute, undercool, cotangent, weight, lift, local, bias, proj,
+    dims, ready, phase, solute, undercool, cotangent, weight, lift, local, bias, proj,
     zf, zg, zi, tx, ty, tyi, txi, txf, tyf,
-    phase_out, solute_out, predicted_out, spectral_out, local_out, proj_out,
+    phase_far, solute_far, predicted_far, modes_far, spec_far, added_far,
+    phase_out, solute_out, predicted_out, spec_out, added_out, out_sem,
     yhi, ylo, from_ylo, from_yhi, from_corner, from_xlo, from_xhi,
-    pad_p, pad_c, pad_d, pad_u, mid_p, mid_c, mid_d, flat, cells, cot, total, coef, lifted, blend, source, field, sums,
+    pad_p, pad_c, pad_d, pad_u, mid_p, mid_c, mid_d, flat, cells, cot, total, coef, lifted, blend, field, sums,
     send1, recv1, send2, recv2, send3, recv3, send4, recv4, recv5, send6, recv6, send7, recv7,
-    send8, recv8, recv9, send10, recv10, send11, recv11, modes,
+    send8, recv8, recv9, send10, recv10, send11, recv11,
     halo_send, halo_recv, send_sem, recv_sem, recv6_sem,
 ):
     gx, gy, group = dims
     ix, iy = lax.axis_index("gx"), lax.axis_index("gy")
     east, west = lax.rem(ix + 1, gx), lax.rem(ix + gx - 1, gx)
     north, south = lax.rem(iy + 1, gy), lax.rem(iy + gy - 1, gy)
-    width = lift.shape[0]
+    width = lift.shape[1]
     pairs = width // 2
     kx, ky = 2 * gx, gy
     square = width * width
@@ -148,6 +179,7 @@
     greet("gx", ix, gx)
     greet("gy", iy, gy)
 
+    ready(0, 1, 2)
     row = iota((8, 8, phase.shape[2]), 1)
     p, c, u = phase[...], solute[...], undercool[...]
     yhi[...] = jnp.where(row >= 6, p, jnp.where(row >= 4, pltpu.roll(c, 6, 1), pltpu.roll(u, 4, 1)))
@@ -156,38 +188,50 @@
     pad_c[2:10, 8:16, :] = c
     pad_u[1:9, 8:16, :] = u
 
-    lane = iota((width, square), 1)
-    inner = lane % width == iota((width, square), 0)
-    for k in range(2):
-        spread = jnp.where(inner, jnp.broadcast_to(lift[:, k : k + 1], (width, square)), 0.0)
-        lifted[k : k + 1, :] = jnp.sum(spread, axis=0, keepdims=True)
-        column = jnp.broadcast_to(lift[:, k : k + 1], (width, 128))
-        coef[k * width : (k + 1) * width] = dot(local[...], column).reshape(width, 1, 128)
-    eye = iota((width, width), 0) == iota((width, width), 1)
-    for k, vector in ((2, bias), (3, proj)):
-        diagonal = jnp.where(eye, jnp.broadcast_to(vector[...], (width, width)), 0.0)
-        coef[k * width : (k + 1) * width] = dot(diagonal, jnp.ones((width, 128), F32)).reshape(width, 1, 128)
-    outer = jnp.where(lane // width == iota((width, square), 0), 1.0, 0.0)
+    depth = phase.shape[2]
     src, dst = iota((128, 128), 0), iota((128, 128), 1)
-    for k in range(2):
-        both = dot(outer, weight[...] * lifted[k : k + 1, :], ((1,), (1,)))
-        for part in range(2):
-            for x in range(2):
-                value = 0.0
-                for par in range(2):
-                    pick = (src % 32 == dst % 32) & (src // 32 == part * 2 + x) & (dst // 64 == par)
-                    value = value + dot(both[par * pairs : (par + 1) * pairs], jnp.where(pick, 1.0, 0.0))
-                blend[2 * k + part, pl.ds(x, pairs, stride=2), :] = value
-    sums[...] = jnp.zeros_like(sums)
-    total[...] = jnp.zeros_like(total)
-    depth = phase.shape[2]
-    for x in range(8):
-        for h in range(2):
-            flat[h, 8 * x : 8 * x + 8, :] = cotangent[x, :, 128 * h : 128 * h + 128]
-    for y in range(8):
-        for h in range(2):
-            cot[8 * y : 8 * y + 8, 128 * h : 128 * h + 128] = flat[h, pl.ds(y, 8, stride=8), :]
-
+    outer = jnp.where(iota((width, square), 1) // width == iota((width, square), 0), 1.0, 0.0)
+
+    def factors_of_channels():
+        ready(5, 6, 7, 8, 3)
+        inner = iota((width, square), 1) % width == iota((width, square), 0)
+        eye = iota((width, width), 0) == iota((width, width), 1)
+
+        def column(v):
+            return jnp.sum(jnp.where(eye, jnp.broadcast_to(v, (width, width)), 0.0), axis=1, keepdims=True)
+
+        for k in range(2):
+            one = column(lift[k : k + 1, :])
+            lifted[k : k + 1, :] = jnp.sum(jnp.where(inner, one, 0.0), axis=0, keepdims=True)
+            mixed = jnp.sum(local[...] * lift[k : k + 1, :], axis=1, keepdims=True)
+            coef[k * width : (k + 1) * width] = jnp.broadcast_to(mixed, (width, 128)).reshape(width, 1, 128)
+        for k, vector in ((2, bias), (3, proj)):
+            one = column(vector[...])
+            coef[k * width : (k + 1) * width] = jnp.broadcast_to(one, (width, 128)).reshape(width, 1, 128)
+        sums[...] = jnp.zeros_like(sums)
+        total[...] = jnp.zeros_like(total)
+        for x in range(8):
+            for h in range(2):
+                flat[h, 8 * x : 8 * x + 8, :] = cotangent[x, :, 128 * h : 128 * h + 128]
+        for y in range(8):
+            for h in range(2):
+                cot[8 * y : 8 * y + 8, 128 * h : 128 * h + 128] = flat[h, pl.ds(y, 8, stride=8), :]
+
+    def weights_of_fields():
+        ready(4)
+        fold = jnp.where(iota((square, width), 0) // width == iota((square, width), 1), 1.0, 0.0)
+        for k in range(2):
+            both = dot_pick(weight[...] * lifted[k : k + 1, :], fold)
+            both = jnp.concatenate([both, jnp.zeros((128, 128 - width), F32)], axis=1).T
+            for part in range(2):
+                for x in range(2):
+                    value = 0.0
+                    for par in range(2):
+                        pick = (src % 32 == dst % 32) & (src // 32 == part * 2 + x) & (dst // 64 == par)
+                        value = value + dot_pick(both[par * pairs : (par + 1) * pairs], jnp.where(pick, 1.0, 0.0))
+                    blend[2 * k + part, pl.ds(x, pairs, stride=2), :] = value
+
+    factors_of_channels()
     pl.semaphore_wait(barrier, 4 + gx - 1 + gy - 1)
 
     def push(source_ref, target_ref, slot, where):
@@ -264,6 +308,9 @@
     lax.fori_loop(0, 12, first_diff, 0)
     lax.fori_loop(0, 10, first, 0)
     lax.fori_loop(0, 8, second, 0)
+    writes = [pltpu.make_async_copy(phase_out, phase_far, out_sem.at[0]), pltpu.make_async_copy(solute_out, solute_far, out_sem.at[1])]
+    for one in writes:
+        one.start()
     for y in range(8):
         for h in range(4):
             cells[8 * y : 8 * y + 8, 128 * h : 128 * h + 128] = flat[h, pl.ds(y, 8, stride=8), :]
@@ -289,13 +336,15 @@
     def arrived(phase_id, whole):
         pltpu.make_async_copy(whole, whole, recv_sem.at[phase_id]).wait()
 
-    along = dot(cells[...], zf[...])
+    ready(9, 12, 13)
+    along = dot_right(cells[...], zf[...])
     lines = jnp.concatenate([along[8 * y : 8 * y + 8] for y in range(8)], axis=1)
     wave = dot(tx[ix].T, lines)
     for y in range(8):
         at = slice(128 * y, 128 * y + 128)
         send1[pl.ds(y, kx, stride=8), :] = wave[:kx, at] + rot(wave[kx:, at])
     exchange("gx", 1, lambda q: send1.at[pl.ds(pl.multiple_of(16 * q, 16), 16)], lambda q: recv1.at[q])
+    weights_of_fields()
     arrived(1, recv1)
     got = recv1[0]
     for q in range(1, gx):
@@ -306,6 +355,7 @@
     exchange("gy", 2, lambda q: send2.at[pl.ds(2 * q, 2)], lambda q: recv2.at[pl.ds(2 * q, 2)])
     arrived(2, recv2)
     got = recv2[...].reshape(gy, 2, 128).sum(0)
+    spec_out[...] = got
 
     even = iota((gy, 128), 0) % 2 == 0
     spread = jnp.where(even, jnp.broadcast_to(got[0:1], (gy, 128)), jnp.broadcast_to(got[1:2], (gy, 128)))
@@ -318,14 +368,10 @@
     send3[...] = value.reshape(gy, 1, 128)
     exchange("gy", 3, lambda q: send3.at[pl.ds(q, 1)], lambda q: recv3.at[pl.ds(q, 1)])
 
-    for x in range(2):
-        diagonal = jnp.where(src == dst, jnp.broadcast_to(got[x : x + 1], (128, 128)), 0.0)
-        column = jnp.sum(diagonal, axis=1, keepdims=True)
-        source[64 * x : 64 * x + 64, :] = column[:64] * lifted[0:1, :] + column[64:] * lifted[1:2, :]
-
     arrived(3, recv3)
     got = recv3[...].reshape(ky, 128)
-    send4[...] = dot(tyi[...], jnp.concatenate([got, rot(got)], axis=0)).reshape(gy, 8, 128)
+    ready(14, 15, 16, 17, 10, 11)
+    send4[...] = dot_left(tyi[...], jnp.concatenate([got, rot(got)], axis=0)).reshape(gy, 8, 128)
     exchange("gy", 4, lambda q: send4.at[q], lambda q: recv4.at[q])
     arrived(4, recv4)
     exchange("gx", 5, lambda q: recv4.at[pl.ds(2 * q, 2)], lambda q: recv5.at[pl.ds(2 * q, 2)])
@@ -334,7 +380,7 @@
     for y in range(8):
         got = recv5[:, y, :]
         lines.append(jnp.concatenate([got, rot(got)], axis=0))
-    wave = dot(txi[...], jnp.concatenate(lines, axis=1))
+    wave = dot_left(txi[...], jnp.concatenate(lines, axis=1))
     for y in range(8):
         send6[:, y] = wave[:, 128 * y : 128 * y + 128].reshape(gx, 8, 128)
 
@@ -363,7 +409,7 @@
         for owner in owners:
             pltpu.make_async_copy(recv6.at[owner], recv6.at[owner], recv6_sem.at[owner]).wait()
         got = jnp.concatenate([recv6[owner].reshape(64, 128) for owner in owners], axis=0)
-        field[...] = dot(got, zi[...])
+        field[...] = dot_right(got, zi[...])
         for t, owner in enumerate(owners):
             factors = [[wide(k * width + par * pairs + owner) for k in range(4)] for par in range(2)]
 
@@ -397,7 +443,7 @@
                 for k in range(3):
                     one = jnp.sum(acc[3 * par + k], axis=0, keepdims=True)
                     sums[k * width + par * pairs + owner] = one[:, :128] + one[:, 128:]
-        wave = dot(field[...], zg[...])
+        wave = dot_right(field[...], zg[...])
         for t, owner in enumerate(owners):
             send7[owner] = wave[64 * t : 64 * t + 64].reshape(8, 8, 128)
 
@@ -424,13 +470,18 @@
     for x in range(8):
         for h in range(2):
             predicted_out[x, :, 128 * h : 128 * h + 128] = flat[h, pl.ds(x, 8, stride=8), :]
+    writes.append(pltpu.make_async_copy(predicted_out, predicted_far, out_sem.at[2]))
     added = dot(jnp.ones((8, 128), F32), sums[...].reshape(128, 128), ((1,), (1,)))
     for q in range(gx):
         send8[24 * q + 16 : 24 * q + 24, :] = added
 
+    writes.append(pltpu.make_async_copy(spec_out, spec_far, out_sem.at[3]))
+    for one in writes[2:]:
+        one.start()
+
     arrived(7, recv7)
     lines = [recv7[:, y].reshape(8 * gx, 128) for y in range(8)]
-    wave = dot(txf[...], jnp.concatenate(lines, axis=1))
+    wave = dot_left(txf[...], jnp.concatenate(lines, axis=1))
     for y in range(8):
         at = slice(128 * y, 128 * y + 128)
         one = wave[:kx, at] + rot(wave[kx:, at])
@@ -447,34 +498,20 @@
     send11[...] = added.reshape(1, 1, 128)
     exchange("gy", 11, lambda q: send11, lambda q: recv11.at[pl.ds(q, 1)])
     arrived(9, recv9)
-    wave = dot(tyf[...], recv9[...].reshape(8 * gy, 128))
+    wave = dot_left(tyf[...], recv9[...].reshape(8 * gy, 128))
     wave = wave[:ky] + rot(wave[ky:])
     send10[...] = wave.reshape(ky, 1, 128)
     exchange("gy", 10, lambda q: send10.at[pl.ds(q, 1)], lambda q: recv10.at[pl.ds(q, 1)])
 
-    scale = 1.0 / math.sqrt(8 * gx * 8 * gy * depth)
     arrived(11, recv11)
-    added = recv11[...].reshape(gy, 128).sum(0, keepdims=True) * scale
-    place = iota((width, 128), 1) - iota((width, 128), 0)
-    value = 0.0
-    for k in range(2):
-        picked = jnp.where(place == k * width, jnp.broadcast_to(added, (width, 128)), 0.0)
-        value = value + jnp.sum(picked, axis=1, keepdims=True) * lifted[k : k + 1, :width]
-    local_out[...] = value
-    pick = iota((128, width), 0) - iota((128, width), 1) == 2 * width
-    proj_out[...] = dot(jnp.broadcast_to(added, (8, 128)), jnp.where(pick, 1.0, 0.0))[0:1]
-
+    added_out[...] = recv11[...].reshape(gy, 128).sum(0, keepdims=True)
+    writes.append(pltpu.make_async_copy(added_out, added_far, out_sem.at[4]))
+    writes[4].start()
     arrived(10, recv10)
-    modes[...] = recv10[...].reshape(gy, 128)
-    for x in range(2):
-        got = modes[pl.ds(x, pairs, stride=2), :]
-        got = jnp.concatenate([got, pltpu.roll(got, 64, 1)], axis=0).T[:64]
-        grad = dot(got, outer)
-        re, im = grad[:32], grad[32:]
-        base = 64 * x
-        s_re, s_im = source[base : base + 32, :], source[base + 32 : base + 64, :]
-        spectral_out[0, x, 0] = re * s_re + im * s_im
-        spectral_out[1, x, 0] = im * s_re - re * s_im
+    writes.append(pltpu.make_async_copy(recv10, modes_far, out_sem.at[5]))
+    writes[5].start()
+    for one in writes:
+        one.wait()
 
     for copy in copies:
         copy.wait_send()
@@ -494,6 +531,65 @@
         pltpu.make_async_copy(whole, whole, send_sem.at[phase_id]).wait()
 
 
+def finish(
+    scale, phase_in, solute_in, predicted_in, modes_in, spec_in, added_in, lift_in,
+    phase_far, solute_far, predicted_far, spectral_far, local_far, proj_far,
+    phase, solute, predicted, modes, spec, added, lift, spectral, local, proj, flat, in_sem, out_sem,
+):
+    far_in = (phase_in, solute_in, predicted_in, modes_in, spec_in, added_in, lift_in)
+    near = (phase, solute, predicted, modes, spec, added, lift)
+    reads = [pltpu.make_async_copy(a, b, in_sem.at[k]) for k, (a, b) in enumerate(zip(far_in, near))]
+    far_out = (phase_far, solute_far, predicted_far, spectral_far, local_far, proj_far)
+    made = (phase, solute, predicted, spectral, local, proj)
+    writes = [pltpu.make_async_copy(a, b, out_sem.at[k]) for k, (a, b) in enumerate(zip(made, far_out))]
+    for k in (6, 4, 3, 5, 0, 1, 2):
+        reads[k].start()
+    width = lift.shape[1]
+    pairs, square = width // 2, width * width
+    outer = jnp.where(iota((width, square), 1) // width == iota((width, square), 0), 1.0, 0.0)
+    inner = iota((width, square), 1) % width == iota((width, square), 0)
+    eye = iota((width, width), 0) == iota((width, width), 1)
+    src, dst = iota((128, 128), 0), iota((128, 128), 1)
+    reads[6].wait()
+    lifted = []
+    for k in range(2):
+        one = jnp.sum(jnp.where(eye, jnp.broadcast_to(lift[k : k + 1, :], (width, width)), 0.0), axis=1, keepdims=True)
+        lifted.append(jnp.sum(jnp.where(inner, one, 0.0), axis=0, keepdims=True))
+    reads[4].wait()
+    reads[3].wait()
+    flat[...] = modes[...].reshape(2 * pairs, 128)
+    for x in range(2):
+        diagonal = jnp.where(src == dst, jnp.broadcast_to(spec[x : x + 1, :], (128, 128)), 0.0)
+        column = jnp.sum(diagonal, axis=1, keepdims=True)
+        source = column[:64] * lifted[0] + column[64:] * lifted[1]
+        got = flat[pl.ds(x, pairs, stride=2), :]
+        got = jnp.concatenate([got, pltpu.roll(got, 64, 1)], axis=0).T[:64]
+        grad = dot_pick(got, outer)
+        re, im = grad[:32], grad[32:]
+        s_re, s_im = source[:32], source[32:]
+        spectral[0, x, 0] = re * s_re + im * s_im
+        spectral[1, x, 0] = im * s_re - re * s_im
+    writes[3].start()
+    for k in range(3):
+        reads[k].wait()
+        writes[k].start()
+    reads[5].wait()
+    scaled = added[...] * scale
+    place = iota((width, 128), 1) - iota((width, 128), 0)
+    value = 0.0
+    for k in range(2):
+        picked = jnp.where(place == k * width, jnp.broadcast_to(scaled, (width, 128)), 0.0)
+        value = value + jnp.sum(picked, axis=1, keepdims=True) * lift[k : k + 1, :]
+    local[...] = value
+    pick = iota((128, width), 0) - iota((128, width), 1) == 2 * width
+    column = jnp.sum(jnp.where(src == dst, jnp.broadcast_to(scaled, (128, 128)), 0.0), axis=1, keepdims=True)
+    proj[...] = jnp.sum(jnp.where(pick, column, 0.0), axis=0, keepdims=True)
+    writes[4].start()
+    writes[5].start()
+    for one in writes:
+        one.wait()
+
+
 def per_device(phase, solute, undercool, lift, weight, local, bias, proj, cotangent):
     gx, gy = lax.axis_size("gx"), lax.axis_size("gy")
     cx, cy, depth = phase.shape
@@ -503,39 +599,66 @@
     assert width == 2 * gx and gy == 2 * gx and (cx, cy, own_kx, own_ky, kz) == (8, 8, 2, 1, 32)
     consts = tables(gx, gy, cx, cy, depth, gx * own_kx, gy * own_ky, kz)
     group = min(4, gx)
-    vmem = pl.BlockSpec(memory_space=pltpu.VMEM)
+    far_spec = pl.BlockSpec(memory_space=pl.ANY)
     buf = lambda *shape: pltpu.VMEM(shape, F32)
     tile = jax.ShapeDtypeStruct((cx, cy, depth), F32)
-    outs = (
-        tile, tile, tile,
-        jax.ShapeDtypeStruct(weight.shape, F32),
-        jax.ShapeDtypeStruct((width, width), F32),
-        jax.ShapeDtypeStruct((1, width), F32),
-    )
+    shape = lambda *dims: jax.ShapeDtypeStruct(dims, F32)
+    outs = (tile, tile, tile, shape(gy, 1, 128), shape(2, 128), shape(1, 128))
     scratch = [
+        buf(8, 8, depth), buf(8, 8, depth), buf(8, 8, depth), buf(2, 128), buf(1, 128), pltpu.SemaphoreType.DMA((6,)),
         buf(8, 8, depth), buf(8, 8, depth), buf(8, 8, depth), buf(8, 8, depth), buf(4, 8, depth), buf(5, 8, depth), buf(5, 8, depth),
         buf(12, 24, depth), buf(12, 24, depth), buf(12, 24, depth), buf(10, 24, depth),
         buf(10, 24, depth), buf(10, 24, depth), buf(10, 24, depth),
         buf(4, 64, 128), buf(64, 2 * depth), buf(64, depth), buf(64, depth),
-        buf(4 * width, 1, 128), buf(2, square), buf(4, gy, 128), buf(128, square), buf(64 * group, 2 * depth), buf(128, 1, 128),
+        buf(4 * width, 1, 128), buf(2, square), buf(4, gy, 128), buf(64 * group, 2 * depth), buf(128, 1, 128),
         buf(16 * gx, 128), buf(gx, 16, 128), buf(2 * gy, 1, 128), buf(2 * gy, 1, 128), buf(gy, 1, 128), buf(gy, 1, 128),
         buf(gy, 8, 128), buf(gy, 8, 128), buf(2 * gx, 8, 128), buf(gx, 8, 8, 128), buf(gx, 8, 8, 128),
         buf(gx, 8, 8, 128), buf(gx, 8, 8, 128), buf(24 * gx, 128), buf(24 * gx, 128), buf(gy, 8, 128),
-        buf(gy, 1, 128), buf(gy, 1, 128), buf(1, 1, 128), buf(gy, 1, 128), buf(gy, 128),
+        buf(gy, 1, 128), buf(gy, 1, 128), buf(1, 1, 128), buf(gy, 1, 128),
         pltpu.SemaphoreType.DMA((12,)), pltpu.SemaphoreType.DMA((12,)),
         pltpu.SemaphoreType.DMA((12,)), pltpu.SemaphoreType.DMA((12,)), pltpu.SemaphoreType.DMA((gx,)),
     ]
-    args = [phase, solute, undercool, cotangent, weight.reshape(128, square), lift, local, bias.reshape(1, -1), proj.reshape(1, -1)]
+    args = [phase, solute, undercool, cotangent, weight.reshape(128, square), lift.T, local, bias.reshape(1, -1), proj.reshape(1, -1)]
     args += [jnp.asarray(t) for t in consts]
+    scratch += [pltpu.VMEM(one.shape, one.dtype) for one in args] + [pltpu.SemaphoreType.DMA((len(args),))]
+    count = len(args)
+
+    def body(*refs):
+        far, rest, near, sems = refs[:count], refs[count : -count - 1], refs[-count - 1 : -1], refs[-1]
+        loads = [pltpu.make_async_copy(far[k], near[k], sems.at[k]) for k in range(count)]
+        for k in (0, 1, 2, 5, 6, 7, 8, 3, 4, 9, 12, 13, 14, 15, 11, 10, 16, 17):
+            loads[k].start()
+
+        def ready(*which):
+            for k in which:
+                loads[k].wait()
+
+        kernel((gx, gy, group), ready, *near, *rest)
+
     got = pl.pallas_call(
-        lambda *refs: kernel((gx, gy, group), *refs),
+        body,
         out_shape=outs,
-        in_specs=[vmem] * len(args),
-        out_specs=(vmem,) * len(outs),
+        in_specs=[far_spec] * count,
+        out_specs=(far_spec,) * len(outs),
         scratch_shapes=scratch,
-        compiler_params=pltpu.CompilerParams(collective_id=0, has_side_effects=True, vmem_limit_bytes=48 * 2**20),
+        compiler_params=pltpu.CompilerParams(collective_id=0, has_side_effects=True, vmem_limit_bytes=60 * 2**20),
         name="layer",
     )(*args)
+    scale = 1.0 / math.sqrt(8 * gx * 8 * gy * depth)
+    finals = (tile, tile, tile, shape(*weight.shape), shape(width, width), shape(1, width))
+    got = pl.pallas_call(
+        lambda *refs: finish(scale, *refs),
+        out_shape=finals,
+        in_specs=[far_spec] * 7,
+        out_specs=(far_spec,) * 6,
+        scratch_shapes=[
+            buf(8, 8, depth), buf(8, 8, depth), buf(8, 8, depth), buf(gy, 1, 128), buf(2, 128), buf(1, 128), buf(2, width),
+            buf(*weight.shape), buf(width, width), buf(1, width), buf(gy, 128),
+            pltpu.SemaphoreType.DMA((7,)), pltpu.SemaphoreType.DMA((6,)),
+        ],
+        compiler_params=pltpu.CompilerParams(vmem_limit_bytes=60 * 2**20),
+        name="finish",
+    )(*got, lift.T)
     return (*got[:5], got[5].reshape(width))
 
 

time: 131 us -> 112 us (0.85)
  local copies, waits for them, and re-layouts: 16.9 us -> 0 us
  Pallas kernels: 113 us -> 110 us
    unnamed x41 -> x0, local copies, waits for them, and re-layouts: 16.9 us -> none
    pallas_call x1 -> x2, Pallas kernels: 113 us -> 110 us  [the longest x1 108 us: per_device(): pl.pallas_call(body, out_shape=outs, in_specs=[far_spec] * count, out_spe...]
where the time goes in v3:
time: 112 us; the launch traced here: 111 us
  Pallas kernels  110 us (98%)
    pallas_call x1, Pallas kernels, per_device(): pl.pallas_call(body, out_shape=outs, in_specs=[far_spec] * count, out_spe...  108 us

profile of v3, /device:TPU:1, one launch (start us, length us, event | category | flops | bytes accessed | tf_op | source)
XLA Modules:
  0.0 110.6 jit_solution(2285180111894194120)
XLA Ops:
  0.6 107.7 %layer.1 = (f32[8,8,256]{2,1,0:T(8,128)}, f32[8,8,256]{2,1,0:T(8,128)}, f32[8,8,256]{2,1,0:T(8,128)}, f32[32,1,128]{2,1,0:T(1,128)}, f32[2,128]{1,0:T(2,128)}, /*index=5*/f32[1,128]{1,0:T(1,128)}) custom-call(f32[8,8,256]{2,1,0:T(8,128)} %refs_0_.1, f32[8,8,256]{2,1,0:T(8,128)} %refs_1_.1, f32[8,8,256]{2,1,0:T(8,128)} %refs_2_.1, f32[8,8,256]{2,1,0:T(8,128)} %refs_3_.1, ...), custom_call_target="tpu_custom_call" | custom-call | tf_op jit(solution)/shard_map/layer/pallas_call | solution.py:638
  108.4 2.2 %finish.1 = (f32[8,8,256]{2,1,0:T(8,128)}, f32[8,8,256]{2,1,0:T(8,128)}, f32[8,8,256]{2,1,0:T(8,128)}, f32[2,2,1,32,1024]{4,3,2,1,0:T(8,128)}, f32[32,32]{1,0:T(8,128)}, /*index=5*/f32[1,32]{1,0:T(1,128)}) custom-call(f32[8,8,256]{2,1,0:T(8,128)} %get-tuple-element.18.refs_0_, f32[8,8,256]{2,1,0:T(8,128)} %get-tuple-element.19.refs_1_, ...), custom_call_target="tpu_custom_call" | custom-call | tf_op jit(solution)/shard_map/finish/pallas_call | solution.py:649

commit v4 on v3

--- a/solution.py
+++ b/solution.py
@@ -61,12 +61,13 @@
     for k in range(own):
         ty[:, k, :, :, :, k] = both
     ty = ty.reshape(gy, own * cy, 2 * ky * own)
-    tyi = np.concatenate([cosy, -siny]).T / ny
+    team = 4 * cy
+    tyi = (np.concatenate([cosy, -siny]).T / ny).reshape(ny // team, team, 2 * ky)
     txi = np.concatenate([cosx, -sinx]).T / nx
     txf = np.stack([cosx, sinx]).reshape(2, gx, own, nx).transpose(0, 2, 1, 3).reshape(2 * kx, nx) / nx
-    tyf = np.concatenate([cosy, siny]) / ny
+    tyf = (np.concatenate([cosy, siny]) / ny).reshape(2 * ky, ny // team, team).transpose(1, 0, 2)
     right = [in_three(t, 0) for t in (zf, zg, zi)]
-    left = [in_three(t, 1) for t in (tyi, txi, txf, tyf)]
+    left = [in_three(t, t.ndim - 1) for t in (tyi, txi, txf, tyf)]
     return right + [np.asarray(tx, np.float32), np.asarray(ty, np.float32)] + left
 
 
@@ -149,11 +150,11 @@
     dims, ready, phase, solute, undercool, cotangent, weight, lift, local, bias, proj,
     zf, zg, zi, tx, ty, tyi, txi, txf, tyf,
     phase_far, solute_far, predicted_far, modes_far, spec_far, added_far,
-    phase_out, solute_out, predicted_out, spec_out, added_out, out_sem,
+    phase_out, solute_out, predicted_out, spec_out, added_out, modes_out, out_sem,
     yhi, ylo, from_ylo, from_yhi, from_corner, from_xlo, from_xhi,
     pad_p, pad_c, pad_d, pad_u, mid_p, mid_c, mid_d, flat, cells, cot, total, coef, lifted, blend, field, sums,
     send1, recv1, send2, recv2, send3, recv3, send4, recv4, recv5, send6, recv6, send7, recv7,
-    send8, recv8, recv9, send10, recv10, send11, recv11,
+    send8, recv8, recv9, send10, recv10, send11, recv11, send12, recv12,
     halo_send, halo_recv, send_sem, recv_sem, recv6_sem,
 ):
     gx, gy, group = dims
@@ -163,6 +164,8 @@
     width = lift.shape[1]
     pairs = width // 2
     kx, ky = 2 * gx, gy
+    rows = gy // 4
+    team, member = iy // 4, lax.rem(iy, 4)
     square = width * width
     barrier = pltpu.get_barrier_semaphore()
 
@@ -200,14 +203,17 @@
         def column(v):
             return jnp.sum(jnp.where(eye, jnp.broadcast_to(v, (width, width)), 0.0), axis=1, keepdims=True)
 
+        def full(v):
+            return jnp.broadcast_to(jnp.broadcast_to(v, (width, 128)).reshape(width, 1, 128), (width, 8, 128))
+
         for k in range(2):
             one = column(lift[k : k + 1, :])
             lifted[k : k + 1, :] = jnp.sum(jnp.where(inner, one, 0.0), axis=0, keepdims=True)
             mixed = jnp.sum(local[...] * lift[k : k + 1, :], axis=1, keepdims=True)
-            coef[k * width : (k + 1) * width] = jnp.broadcast_to(mixed, (width, 128)).reshape(width, 1, 128)
+            coef[k * width : (k + 1) * width] = full(mixed)
         for k, vector in ((2, bias), (3, proj)):
             one = column(vector[...])
-            coef[k * width : (k + 1) * width] = jnp.broadcast_to(one, (width, 128)).reshape(width, 1, 128)
+            coef[k * width : (k + 1) * width] = full(one)
         sums[...] = jnp.zeros_like(sums)
         total[...] = jnp.zeros_like(total)
         for x in range(8):
@@ -316,7 +322,7 @@
             cells[8 * y : 8 * y + 8, 128 * h : 128 * h + 128] = flat[h, pl.ds(y, 8, stride=8), :]
 
     def exchange(axis, phase_id, sends, receives):
-        mine, count = (ix, gx) if axis == "gx" else (iy, gy)
+        mine, count = {"gx": (ix, gx), "gy": (iy, gy), "team": (member, 4)}[axis]
         pltpu.make_async_copy(sends(mine), receives(mine), recv_sem.at[phase_id]).start()
 
         def one(j, carry):
@@ -326,7 +332,7 @@
                 dst_ref=receives(mine),
                 send_sem=send_sem.at[phase_id],
                 recv_sem=recv_sem.at[phase_id],
-                device_id={axis: peer},
+                device_id={"gy": 4 * team + peer} if axis == "team" else {axis: peer},
                 device_id_type=MESH,
             ).start()
             return carry
@@ -365,14 +371,19 @@
     for k in range(2):
         one = jnp.where(low, spread, turned) if k == 0 else jnp.where(low, turned, spread)
         value = value + blend[2 * k] * one - blend[2 * k + 1] * rot(one)
-    send3[...] = value.reshape(gy, 1, 128)
-    exchange("gy", 3, lambda q: send3.at[pl.ds(q, 1)], lambda q: recv3.at[pl.ds(q, 1)])
+    send3[...] = value.reshape(4, rows, 128)
+    exchange("gy", 3, lambda q: send3.at[lax.rem(q, 4)], lambda q: recv3.at[pl.ds(pl.multiple_of(rows * q, rows), rows)])
+    ready(14, 15, 16, 17, 10, 11)
 
     arrived(3, recv3)
-    got = recv3[...].reshape(ky, 128)
-    ready(14, 15, 16, 17, 10, 11)
-    send4[...] = dot_left(tyi[...], jnp.concatenate([got, rot(got)], axis=0)).reshape(gy, 8, 128)
-    exchange("gy", 4, lambda q: send4.at[q], lambda q: recv4.at[q])
+    lines = []
+    for r in range(rows):
+        got = recv3[pl.ds(r, ky, stride=rows), :]
+        lines.append(jnp.concatenate([got, rot(got)], axis=0))
+    wave = dot_left(tyi[team], jnp.concatenate(lines, axis=1))
+    for r in range(rows):
+        send4[:, r] = wave[:, 128 * r : 128 * r + 128].reshape(4, 8, 128)
+    exchange("team", 4, lambda q: send4.at[q], lambda q: recv4.at[pl.ds(rows * q, rows)])
     arrived(4, recv4)
     exchange("gx", 5, lambda q: recv4.at[pl.ds(2 * q, 2)], lambda q: recv5.at[pl.ds(2 * q, 2)])
     arrived(5, recv5)
@@ -401,8 +412,8 @@
     lax.fori_loop(1, gx, give, 0)
 
     def wide(o):
-        one = coef[o]
-        return jnp.concatenate([one, one], axis=1)
+        one = jnp.concatenate([coef[o], coef[o]], axis=1)
+        return jnp.concatenate([one, one], axis=0)
 
     def step(j, carry):
         owners = [lax.rem(ix + gx - (j * group + t), gx) for t in range(group)]
@@ -411,34 +422,30 @@
         got = jnp.concatenate([recv6[owner].reshape(64, 128) for owner in owners], axis=0)
         field[...] = dot_right(got, zi[...])
         for t, owner in enumerate(owners):
-            factors = [[wide(k * width + par * pairs + owner) for k in range(4)] for par in range(2)]
-
             def block(r, acc):
-                at = pl.multiple_of(8 * r, 8)
-                here = pl.ds(pl.multiple_of(64 * t + 8 * r, 8), 8)
-                p, c, w = cells[pl.ds(at, 8), :depth], cells[pl.ds(at, 8), depth:], cot[pl.ds(at, 8), :]
+                at = pl.ds(pl.multiple_of(16 * r, 16), 16)
+                here = pl.ds(pl.multiple_of(64 * t + 16 * r, 16), 16)
+                p, c, w = cells[at, :depth], cells[at, depth:], cot[at, :]
                 acc = list(acc)
-                out = total[pl.ds(at, 8), :]
+                out = total[at, :]
                 for par in range(2):
-                    m0, m1, b, q = factors[par]
+                    m0, m1, b, q = (wide(k * width + par * pairs + owner) for k in range(4))
                     side = slice(par * depth, (par + 1) * depth)
                     pre = field[here, side] + m0 * p + m1 * c + b
                     power = pre * pre
-                    tanh = jnp.tanh(GELU_K * (pre + GELU_C * (power * pre)))
-                    half = 0.5 * (1.0 + tanh)
+                    half = 0.5 + 0.5 * jnp.tanh(pre * (GELU_K + (GELU_K * GELU_C) * power))
                     act = pre * half
-                    slope = half + (0.5 * GELU_K) * pre * (1.0 - tanh * tanh) * (1.0 + (3.0 * GELU_C) * power)
+                    slope = half + act * (1.0 - half) * (2.0 * GELU_K + (6.0 * GELU_K * GELU_C) * power)
                     out = out + q * act
                     grad = q * w * slope
                     field[here, side] = grad
-                    acc[3 * par] = acc[3 * par] + grad * p
-                    acc[3 * par + 1] = acc[3 * par + 1] + grad * c
-                    acc[3 * par + 2] = acc[3 * par + 2] + act * w
-                total[pl.ds(at, 8), :] = out
+                    for k, v in enumerate((grad * p, grad * c, act * w)):
+                        acc[3 * par + k] = acc[3 * par + k] + (v[:8] + v[8:])
+                total[at, :] = out
                 return tuple(acc)
 
             zero = jnp.zeros((8, depth), F32)
-            acc = lax.fori_loop(0, 8, block, (zero,) * 6)
+            acc = lax.fori_loop(0, 4, block, (zero,) * 6)
             for par in range(2):
                 for k in range(3):
                     one = jnp.sum(acc[3 * par + k], axis=0, keepdims=True)
@@ -472,9 +479,8 @@
             predicted_out[x, :, 128 * h : 128 * h + 128] = flat[h, pl.ds(x, 8, stride=8), :]
     writes.append(pltpu.make_async_copy(predicted_out, predicted_far, out_sem.at[2]))
     added = dot(jnp.ones((8, 128), F32), sums[...].reshape(128, 128), ((1,), (1,)))
-    for q in range(gx):
-        send8[24 * q + 16 : 24 * q + 24, :] = added
-
+    send12[...] = added[0:1].reshape(1, 1, 128)
+    exchange("gx", 12, lambda q: send12, lambda q: recv12.at[pl.ds(q, 1)])
     writes.append(pltpu.make_async_copy(spec_out, spec_far, out_sem.at[3]))
     for one in writes[2:]:
         one.start()
@@ -486,29 +492,38 @@
         at = slice(128 * y, 128 * y + 128)
         one = wave[:kx, at] + rot(wave[kx:, at])
         for k in range(2):
-            send8[pl.ds(8 * k + y, gx, stride=24), :] = one[k * gx : (k + 1) * gx]
-    exchange("gx", 8, lambda q: send8.at[pl.ds(pl.multiple_of(24 * q, 8), 24)], lambda q: recv8.at[pl.ds(pl.multiple_of(24 * q, 8), 24)])
+            send8[pl.ds(8 * k + y, gx, stride=16), :] = one[k * gx : (k + 1) * gx]
+    exchange("gx", 8, lambda q: send8.at[pl.ds(pl.multiple_of(16 * q, 16), 16)], lambda q: recv8.at[pl.ds(pl.multiple_of(16 * q, 16), 16)])
+    arrived(12, recv12)
+    send11[...] = recv12[...].reshape(gx, 128).sum(0, keepdims=True).reshape(1, 1, 128)
+    exchange("gy", 11, lambda q: send11, lambda q: recv11.at[pl.ds(q, 1)])
     arrived(8, recv8)
-
-    def part(q):
-        return recv8.at[pl.ds(pl.multiple_of(24 * (q // 2) + 8 * (q % 2), 8), 8)]
-
-    exchange("gy", 9, part, lambda q: recv9.at[q])
-    added = recv8[pl.ds(16, gx, stride=24), :].sum(0, keepdims=True)
-    send11[...] = added.reshape(1, 1, 128)
-    exchange("gy", 11, lambda q: send11, lambda q: recv11.at[pl.ds(q, 1)])
+    block = 8 * rows
+    exchange(
+        "team", 9,
+        lambda q: recv8.at[pl.ds(pl.multiple_of(block * q, block), block)],
+        lambda q: recv9.at[pl.ds(pl.multiple_of(block * q, block), block)],
+    )
     arrived(9, recv9)
-    wave = dot_left(tyf[...], recv9[...].reshape(8 * gy, 128))
-    wave = wave[:ky] + rot(wave[ky:])
-    send10[...] = wave.reshape(ky, 1, 128)
-    exchange("gy", 10, lambda q: send10.at[pl.ds(q, 1)], lambda q: recv10.at[pl.ds(q, 1)])
-
+    lines = []
+    for r in range(rows):
+        lines.append(jnp.concatenate([recv9[block * m + 8 * r : block * m + 8 * r + 8] for m in range(4)], axis=0))
+    wave = dot_left(tyf[team], jnp.concatenate(lines, axis=1))
+    for r in range(rows):
+        at = slice(128 * r, 128 * r + 128)
+        send10[pl.ds(r, ky, stride=rows), :] = wave[:ky, at] + rot(wave[ky:, at])
+    part = lambda ref: lambda q: ref.at[pl.ds(pl.multiple_of(rows * q, rows), rows)]
+    exchange("gy", 10, part(send10), part(recv10))
     arrived(11, recv11)
     added_out[...] = recv11[...].reshape(gy, 128).sum(0, keepdims=True)
     writes.append(pltpu.make_async_copy(added_out, added_far, out_sem.at[4]))
     writes[4].start()
     arrived(10, recv10)
-    writes.append(pltpu.make_async_copy(recv10, modes_far, out_sem.at[5]))
+    got = recv10[0:gy]
+    for g in range(1, gy // 4):
+        got = got + recv10[gy * g : gy * g + gy]
+    modes_out[...] = got
+    writes.append(pltpu.make_async_copy(modes_out, modes_far, out_sem.at[5]))
     writes[5].start()
     for one in writes:
         one.wait()
@@ -518,15 +533,16 @@
     for phase_id, whole in (
         (1, recv1.at[1:gx]),
         (2, send2.at[2 : 2 * gy]),
-        (3, send3.at[1:gy]),
-        (4, send4.at[1:gy]),
+        (3, recv3.at[rows : gy * rows]),
+        (4, recv4.at[rows:gy]),
         (5, recv4.at[2 : 2 * gx]),
         (6, send6.at[1:gx]),
         (7, send7.at[1:gx]),
-        (8, send8.at[24 : 24 * gx]),
-        (9, recv9.at[1:gy]),
-        (10, send10.at[1:gy]),
+        (8, send8.at[16 : 16 * gx]),
+        (9, recv9.at[block : 4 * block]),
+        (10, send10.at[rows : gy * rows]),
         (11, recv11.at[1:gy]),
+        (12, recv12.at[1:gx]),
     ):
         pltpu.make_async_copy(whole, whole, send_sem.at[phase_id]).wait()
 
@@ -534,7 +550,7 @@
 def finish(
     scale, phase_in, solute_in, predicted_in, modes_in, spec_in, added_in, lift_in,
     phase_far, solute_far, predicted_far, spectral_far, local_far, proj_far,
-    phase, solute, predicted, modes, spec, added, lift, spectral, local, proj, flat, in_sem, out_sem,
+    phase, solute, predicted, modes, spec, added, lift, spectral, local, proj, in_sem, out_sem,
 ):
     far_in = (phase_in, solute_in, predicted_in, modes_in, spec_in, added_in, lift_in)
     near = (phase, solute, predicted, modes, spec, added, lift)
@@ -557,12 +573,11 @@
         lifted.append(jnp.sum(jnp.where(inner, one, 0.0), axis=0, keepdims=True))
     reads[4].wait()
     reads[3].wait()
-    flat[...] = modes[...].reshape(2 * pairs, 128)
     for x in range(2):
         diagonal = jnp.where(src == dst, jnp.broadcast_to(spec[x : x + 1, :], (128, 128)), 0.0)
         column = jnp.sum(diagonal, axis=1, keepdims=True)
         source = column[:64] * lifted[0] + column[64:] * lifted[1]
-        got = flat[pl.ds(x, pairs, stride=2), :]
+        got = modes[pl.ds(x, pairs, stride=2), :]
         got = jnp.concatenate([got, pltpu.roll(got, 64, 1)], axis=0).T[:64]
         grad = dot_pick(got, outer)
         re, im = grad[:32], grad[32:]
@@ -598,25 +613,25 @@
     square = width * width
     assert width == 2 * gx and gy == 2 * gx and (cx, cy, own_kx, own_ky, kz) == (8, 8, 2, 1, 32)
     consts = tables(gx, gy, cx, cy, depth, gx * own_kx, gy * own_ky, kz)
-    group = min(4, gx)
+    group, rows = min(4, gx), gy // 4
     far_spec = pl.BlockSpec(memory_space=pl.ANY)
     buf = lambda *shape: pltpu.VMEM(shape, F32)
     tile = jax.ShapeDtypeStruct((cx, cy, depth), F32)
     shape = lambda *dims: jax.ShapeDtypeStruct(dims, F32)
-    outs = (tile, tile, tile, shape(gy, 1, 128), shape(2, 128), shape(1, 128))
+    outs = (tile, tile, tile, shape(gy, 128), shape(2, 128), shape(1, 128))
     scratch = [
-        buf(8, 8, depth), buf(8, 8, depth), buf(8, 8, depth), buf(2, 128), buf(1, 128), pltpu.SemaphoreType.DMA((6,)),
+        buf(8, 8, depth), buf(8, 8, depth), buf(8, 8, depth), buf(2, 128), buf(1, 128), buf(gy, 128), pltpu.SemaphoreType.DMA((6,)),
         buf(8, 8, depth), buf(8, 8, depth), buf(8, 8, depth), buf(8, 8, depth), buf(4, 8, depth), buf(5, 8, depth), buf(5, 8, depth),
         buf(12, 24, depth), buf(12, 24, depth), buf(12, 24, depth), buf(10, 24, depth),
         buf(10, 24, depth), buf(10, 24, depth), buf(10, 24, depth),
         buf(4, 64, 128), buf(64, 2 * depth), buf(64, depth), buf(64, depth),
-        buf(4 * width, 1, 128), buf(2, square), buf(4, gy, 128), buf(64 * group, 2 * depth), buf(128, 1, 128),
-        buf(16 * gx, 128), buf(gx, 16, 128), buf(2 * gy, 1, 128), buf(2 * gy, 1, 128), buf(gy, 1, 128), buf(gy, 1, 128),
-        buf(gy, 8, 128), buf(gy, 8, 128), buf(2 * gx, 8, 128), buf(gx, 8, 8, 128), buf(gx, 8, 8, 128),
-        buf(gx, 8, 8, 128), buf(gx, 8, 8, 128), buf(24 * gx, 128), buf(24 * gx, 128), buf(gy, 8, 128),
-        buf(gy, 1, 128), buf(gy, 1, 128), buf(1, 1, 128), buf(gy, 1, 128),
+        buf(4 * width, 8, 128), buf(2, square), buf(4, gy, 128), buf(64 * group, 2 * depth), buf(128, 1, 128),
+        buf(16 * gx, 128), buf(gx, 16, 128), buf(2 * gy, 1, 128), buf(2 * gy, 1, 128), buf(4, rows, 128), buf(gy * rows, 128),
+        buf(4, rows, 8, 128), buf(gy, 8, 128), buf(2 * gx, 8, 128), buf(gx, 8, 8, 128), buf(gx, 8, 8, 128),
+        buf(gx, 8, 8, 128), buf(gx, 8, 8, 128), buf(16 * gx, 128), buf(16 * gx, 128), buf(32 * rows, 128),
+        buf(gy * rows, 128), buf(gy * rows, 128), buf(1, 1, 128), buf(gy, 1, 128), buf(1, 1, 128), buf(gx, 1, 128),
         pltpu.SemaphoreType.DMA((12,)), pltpu.SemaphoreType.DMA((12,)),
-        pltpu.SemaphoreType.DMA((12,)), pltpu.SemaphoreType.DMA((12,)), pltpu.SemaphoreType.DMA((gx,)),
+        pltpu.SemaphoreType.DMA((13,)), pltpu.SemaphoreType.DMA((13,)), pltpu.SemaphoreType.DMA((gx,)),
     ]
     args = [phase, solute, undercool, cotangent, weight.reshape(128, square), lift.T, local, bias.reshape(1, -1), proj.reshape(1, -1)]
     args += [jnp.asarray(t) for t in consts]
@@ -652,8 +667,8 @@
         in_specs=[far_spec] * 7,
         out_specs=(far_spec,) * 6,
         scratch_shapes=[
-            buf(8, 8, depth), buf(8, 8, depth), buf(8, 8, depth), buf(gy, 1, 128), buf(2, 128), buf(1, 128), buf(2, width),
-            buf(*weight.shape), buf(width, width), buf(1, width), buf(gy, 128),
+            buf(8, 8, depth), buf(8, 8, depth), buf(8, 8, depth), buf(gy, 128), buf(2, 128), buf(1, 128), buf(2, width),
+            buf(*weight.shape), buf(width, width), buf(1, width),
             pltpu.SemaphoreType.DMA((7,)), pltpu.SemaphoreType.DMA((6,)),
         ],
         compiler_params=pltpu.CompilerParams(vmem_limit_bytes=60 * 2**20),

time: 112 us -> 102 us (0.911); the launches traced: 111 us -> 102 us
  Pallas kernels: 110 us -> 101 us
    pallas_call x1, Pallas kernels: 108 us -> 99.1 us  [per_device(): pl.pallas_call(body, out_shape=outs, in_specs=[far_spec] * count, out_spe...]
where the time goes in v4:
time: 102 us
  Pallas kernels  101 us (99%)
    pallas_call x1, Pallas kernels, per_device(): pl.pallas_call(body, out_shape=outs, in_specs=[far_spec] * count, out_spe...  99.1 us
    pallas_call x1, Pallas kernels, per_device(): pl.pallas_call(lambda *refs: finish(scale, *refs), out_shape=finals, in_s...  2.17 us

profile of v4, /device:TPU:1, one launch (start us, length us, event | category | flops | bytes accessed | tf_op | source)
XLA Modules:
  0.0 101.9 jit_solution(2675038677274940052)
XLA Ops:
  0.6 99.1 %layer.1 = (f32[8,8,256]{2,1,0:T(8,128)}, f32[8,8,256]{2,1,0:T(8,128)}, f32[8,8,256]{2,1,0:T(8,128)}, f32[32,128]{1,0:T(8,128)}, f32[2,128]{1,0:T(2,128)}, /*index=5*/f32[1,128]{1,0:T(1,128)}) custom-call(f32[8,8,256]{2,1,0:T(8,128)} %refs_0_.1, f32[8,8,256]{2,1,0:T(8,128)} %refs_1_.1, f32[8,8,256]{2,1,0:T(8,128)} %refs_2_.1, f32[8,8,256]{2,1,0:T(8,128)} %refs_3_.1, ...), custom_call_target="tpu_custom_call" | custom-call | tf_op jit(solution)/shard_map/layer/pallas_call | solution.py:653
  99.7 2.2 %finish.1 = (f32[8,8,256]{2,1,0:T(8,128)}, f32[8,8,256]{2,1,0:T(8,128)}, f32[8,8,256]{2,1,0:T(8,128)}, f32[2,2,1,32,1024]{4,3,2,1,0:T(8,128)}, f32[32,32]{1,0:T(8,128)}, /*index=5*/f32[1,32]{1,0:T(1,128)}) custom-call(f32[8,8,256]{2,1,0:T(8,128)} %get-tuple-element.18.refs_0_, f32[8,8,256]{2,1,0:T(8,128)} %get-tuple-element.19.refs_1_, ...), custom_call_target="tpu_custom_call" | custom-call | tf_op jit(solution)/shard_map/finish/pallas_call | solution.py:664

commit v5 on v4

--- a/solution.py
+++ b/solution.py
@@ -146,8 +146,30 @@
     return p + TIME_STEP * rate, c + TIME_STEP * (div + 0.5 * (1.0 - keff) * c * rate)
 
 
+def partners(ix, gx, sign):
+    if gx != 16:
+        steps = [lax.rem(ix + gx + sign * k, gx) for k in range(gx)]
+        return steps, None
+    x, y, core = ix // 8, lax.rem(ix // 2, 4), lax.rem(ix, 2)
+    xs = [8 * x, 8 * (1 - x)]
+    ys = [2 * lax.rem(y + 4 + sign * d, 4) for d in range(4)]
+    cores = [core, 1 - core]
+    steps = [xs[dx] + ys[dy] + cores[c] for dx, dy in ((0, 0), (1, 0), (0, 2), (1, 2), (1, 1), (1, 3), (0, 1), (0, 3)) for c in range(2)]
+
+    def group(j):
+        found = []
+        for b in range(2):
+            dx = jnp.where(j < 2, b, 3 - j)
+            dy = jnp.where(j < 2, 2 * j, 1 + 2 * b)
+            at = jnp.where(dx == 1, xs[1], xs[0]) + 2 * lax.rem(y + 4 + sign * dy, 4)
+            found += [at + cores[0], at + cores[1]]
+        return found
+
+    return steps, group
+
+
 def kernel(
-    dims, ready, phase, solute, undercool, cotangent, weight, lift, local, bias, proj,
+    dims, start, ready, phase, solute, undercool, cotangent, weight, lift, local, bias, proj,
     zf, zg, zi, tx, ty, tyi, txi, txf, tyf,
     phase_far, solute_far, predicted_far, modes_far, spec_far, added_far,
     phase_out, solute_out, predicted_out, spec_out, added_out, modes_out, out_sem,
@@ -167,20 +189,30 @@
     rows = gy // 4
     team, member = iy // 4, lax.rem(iy, 4)
     square = width * width
+    outward, _ = partners(ix, gx, 1)
+    inward, inward_group = partners(ix, gx, -1)
+    assert inward_group or gx <= group
     barrier = pltpu.get_barrier_semaphore()
 
-    def greet(axis, mine, count):
-        def one(j, carry):
-            pl.semaphore_signal(barrier, inc=1, device_id={axis: lax.rem(mine + j, count)}, device_id_type=MESH)
-            return carry
-
-        lax.fori_loop(1, count, one, 0)
-
+    def greet(where):
+        pl.semaphore_signal(barrier, inc=1, device_id=where, device_id_type=MESH)
+
+    def greet_y(k, carry):
+        greet({"gy": lax.rem(iy + gy // 2 + k, gy)})
+        greet({"gy": lax.rem(iy + gy // 2 + gy - k, gy)})
+        return carry
+
+    def greet_x(j, carry):
+        greet({"gx": lax.rem(ix + j, gx)})
+        return carry
+
+    greet({"gy": lax.rem(iy + gy // 2, gy)})
+    lax.fori_loop(1, gy // 2, greet_y, 0)
     for a in (east, west):
         for b in (north, south):
-            pl.semaphore_signal(barrier, inc=1, device_id={"gx": a, "gy": b}, device_id_type=MESH)
-    greet("gx", ix, gx)
-    greet("gy", iy, gy)
+            greet({"gx": a, "gy": b})
+    lax.fori_loop(1, gx, greet_x, 0)
+    start()
 
     ready(0, 1, 2)
     row = iota((8, 8, phase.shape[2]), 1)
@@ -325,8 +357,7 @@
         mine, count = {"gx": (ix, gx), "gy": (iy, gy), "team": (member, 4)}[axis]
         pltpu.make_async_copy(sends(mine), receives(mine), recv_sem.at[phase_id]).start()
 
-        def one(j, carry):
-            peer = lax.rem(mine + j, count)
+        def to(peer):
             pltpu.make_async_remote_copy(
                 src_ref=sends(peer),
                 dst_ref=receives(mine),
@@ -335,9 +366,21 @@
                 device_id={"gy": 4 * team + peer} if axis == "team" else {axis: peer},
                 device_id_type=MESH,
             ).start()
+
+        def both_ways(k, carry):
+            to(lax.rem(iy + gy // 2 + k, gy))
+            to(lax.rem(iy + gy // 2 + gy - k, gy))
             return carry
 
-        lax.fori_loop(1, count, one, 0)
+        if axis == "gy":
+            to(lax.rem(iy + gy // 2, gy))
+            lax.fori_loop(1, gy // 2, both_ways, 0)
+        elif axis == "gx":
+            for k in range(1, gx):
+                to(outward[1 + (k + 2) % (gx - 1)])
+        else:
+            for k in (2, 1, 3):
+                to(lax.rem(member + k, 4))
 
     def arrived(phase_id, whole):
         pltpu.make_async_copy(whole, whole, recv_sem.at[phase_id]).wait()
@@ -397,8 +440,7 @@
 
     pltpu.make_async_copy(send6.at[ix], recv6.at[ix], recv6_sem.at[ix]).start()
 
-    def give(j, carry):
-        peer = lax.rem(ix + j, gx)
+    for peer in outward[1:]:
         pltpu.make_async_remote_copy(
             src_ref=send6.at[peer],
             dst_ref=recv6.at[ix],
@@ -407,16 +449,13 @@
             device_id={"gx": peer},
             device_id_type=MESH,
         ).start()
-        return carry
-
-    lax.fori_loop(1, gx, give, 0)
 
     def wide(o):
         one = jnp.concatenate([coef[o], coef[o]], axis=1)
         return jnp.concatenate([one, one], axis=0)
 
     def step(j, carry):
-        owners = [lax.rem(ix + gx - (j * group + t), gx) for t in range(group)]
+        owners = inward_group(j) if inward_group else inward
         for owner in owners:
             pltpu.make_async_copy(recv6.at[owner], recv6.at[owner], recv6_sem.at[owner]).wait()
         got = jnp.concatenate([recv6[owner].reshape(64, 128) for owner in owners], axis=0)
@@ -641,14 +680,16 @@
     def body(*refs):
         far, rest, near, sems = refs[:count], refs[count : -count - 1], refs[-count - 1 : -1], refs[-1]
         loads = [pltpu.make_async_copy(far[k], near[k], sems.at[k]) for k in range(count)]
-        for k in (0, 1, 2, 5, 6, 7, 8, 3, 4, 9, 12, 13, 14, 15, 11, 10, 16, 17):
-            loads[k].start()
+
+        def start():
+            for k in (0, 1, 2, 5, 6, 7, 8, 3, 4, 9, 12, 13, 14, 15, 11, 10, 16, 17):
+                loads[k].start()
 
         def ready(*which):
             for k in which:
                 loads[k].wait()
 
-        kernel((gx, gy, group), ready, *near, *rest)
+        kernel((gx, gy, group), start, ready, *near, *rest)
 
     got = pl.pallas_call(
         body,

time: 102 us -> 97.4 us (0.955)
  Pallas kernels: 101 us -> 95.9 us
    pallas_call x1, Pallas kernels: 99.1 us -> 93.7 us  [per_device(): pl.pallas_call(body, out_shape=outs, in_specs=[far_spec] * count, out_spe...]
where the time goes in v5:
time: 97.4 us; the launch traced here: 96.6 us
  Pallas kernels  95.9 us (98%)
    pallas_call x1, Pallas kernels, per_device(): pl.pallas_call(body, out_shape=outs, in_specs=[far_spec] * count, out_spe...  93.7 us
    pallas_call x1, Pallas kernels, per_device(): pl.pallas_call(lambda *refs: finish(scale, *refs), out_shape=finals, in_s...  2.18 us

profile of v5, /device:TPU:1, one launch (start us, length us, event | category | flops | bytes accessed | tf_op | source)
XLA Modules:
  0.0 96.6 jit_solution(17731466452535965022)
XLA Ops:
  0.6 93.7 %layer.1 = (f32[8,8,256]{2,1,0:T(8,128)}, f32[8,8,256]{2,1,0:T(8,128)}, f32[8,8,256]{2,1,0:T(8,128)}, f32[32,128]{1,0:T(8,128)}, f32[2,128]{1,0:T(2,128)}, /*index=5*/f32[1,128]{1,0:T(1,128)}) custom-call(f32[8,8,256]{2,1,0:T(8,128)} %refs_0_.1, f32[8,8,256]{2,1,0:T(8,128)} %refs_1_.1, f32[8,8,256]{2,1,0:T(8,128)} %refs_2_.1, f32[8,8,256]{2,1,0:T(8,128)} %refs_3_.1, ...), custom_call_target="tpu_custom_call" | custom-call | tf_op jit(solution)/shard_map/layer/pallas_call | solution.py:694
  94.4 2.2 %finish.1 = (f32[8,8,256]{2,1,0:T(8,128)}, f32[8,8,256]{2,1,0:T(8,128)}, f32[8,8,256]{2,1,0:T(8,128)}, f32[2,2,1,32,1024]{4,3,2,1,0:T(8,128)}, f32[32,32]{1,0:T(8,128)}, /*index=5*/f32[1,32]{1,0:T(1,128)}) custom-call(f32[8,8,256]{2,1,0:T(8,128)} %get-tuple-element.18.refs_0_, f32[8,8,256]{2,1,0:T(8,128)} %get-tuple-element.19.refs_1_, ...), custom_call_target="tpu_custom_call" | custom-call | tf_op jit(solution)/shard_map/finish/pallas_call | solution.py:705

commit v6 on v5

--- a/solution.py
+++ b/solution.py
@@ -175,8 +175,8 @@
     phase_out, solute_out, predicted_out, spec_out, added_out, modes_out, out_sem,
     yhi, ylo, from_ylo, from_yhi, from_corner, from_xlo, from_xhi,
     pad_p, pad_c, pad_d, pad_u, mid_p, mid_c, mid_d, flat, cells, cot, total, coef, lifted, blend, field, sums,
-    send1, recv1, send2, recv2, send3, recv3, send4, recv4, recv5, send6, recv6, send7, recv7,
-    send8, recv8, recv9, send10, recv10, send11, recv11, send12, recv12,
+    send1, recv1, send2, recv2, send3, recv3, send4, recv5, send6, recv6, send7, recv7,
+    send8, recv9, send10, recv10, send11, recv11, send12, recv12,
     halo_send, halo_recv, send_sem, recv_sem, recv6_sem,
 ):
     gx, gy, group = dims
@@ -188,6 +188,9 @@
     kx, ky = 2 * gx, gy
     rows = gy // 4
     team, member = iy // 4, lax.rem(iy, 4)
+    per = gx // 4
+    holder = ix // per
+    same = holder == member
     square = width * width
     outward, _ = partners(ix, gx, 1)
     inward, inward_group = partners(ix, gx, -1)
@@ -212,6 +215,18 @@
         for b in (north, south):
             greet({"gx": a, "gy": b})
     lax.fori_loop(1, gx, greet_x, 0)
+
+    def greet_holders(q, carry):
+        greet({"gx": q, "gy": 4 * team + holder})
+        return carry
+
+    def greet_owners(a, carry):
+        for m in range(4):
+            greet({"gx": per * member + a, "gy": 4 * team + m})
+        return carry
+
+    lax.fori_loop(0, gx, greet_holders, 0)
+    lax.fori_loop(0, per, greet_owners, 0)
     start()
 
     ready(0, 1, 2)
@@ -270,7 +285,7 @@
                     blend[2 * k + part, pl.ds(x, pairs, stride=2), :] = value
 
     factors_of_channels()
-    pl.semaphore_wait(barrier, 4 + gx - 1 + gy - 1)
+    pl.semaphore_wait(barrier, 4 + gx - 1 + gy - 1 + 2 * gx)
 
     def push(source_ref, target_ref, slot, where):
         copy = pltpu.make_async_remote_copy(
@@ -354,7 +369,7 @@
             cells[8 * y : 8 * y + 8, 128 * h : 128 * h + 128] = flat[h, pl.ds(y, 8, stride=8), :]
 
     def exchange(axis, phase_id, sends, receives):
-        mine, count = {"gx": (ix, gx), "gy": (iy, gy), "team": (member, 4)}[axis]
+        mine = ix if axis == "gx" else iy
         pltpu.make_async_copy(sends(mine), receives(mine), recv_sem.at[phase_id]).start()
 
         def to(peer):
@@ -363,7 +378,7 @@
                 dst_ref=receives(mine),
                 send_sem=send_sem.at[phase_id],
                 recv_sem=recv_sem.at[phase_id],
-                device_id={"gy": 4 * team + peer} if axis == "team" else {axis: peer},
+                device_id={axis: peer},
                 device_id_type=MESH,
             ).start()
 
@@ -375,12 +390,26 @@
         if axis == "gy":
             to(lax.rem(iy + gy // 2, gy))
             lax.fori_loop(1, gy // 2, both_ways, 0)
-        elif axis == "gx":
+        else:
             for k in range(1, gx):
                 to(outward[1 + (k + 2) % (gx - 1)])
+
+    def straight(phase_id, source_ref, target_ref, q, m, own):
+        def far():
+            pltpu.make_async_remote_copy(
+                src_ref=source_ref,
+                dst_ref=target_ref,
+                send_sem=send_sem.at[phase_id],
+                recv_sem=recv_sem.at[phase_id],
+                device_id={"gx": q, "gy": 4 * team + m},
+                device_id_type=MESH,
+            ).start()
+
+        if own is None:
+            far()
         else:
-            for k in (2, 1, 3):
-                to(lax.rem(member + k, 4))
+            pl.when(own)(lambda: pltpu.make_async_copy(source_ref, target_ref, recv_sem.at[phase_id]).start())
+            pl.when(jnp.logical_not(own))(far)
 
     def arrived(phase_id, whole):
         pltpu.make_async_copy(whole, whole, recv_sem.at[phase_id]).wait()
@@ -426,10 +455,12 @@
     wave = dot_left(tyi[team], jnp.concatenate(lines, axis=1))
     for r in range(rows):
         send4[:, r] = wave[:, 128 * r : 128 * r + 128].reshape(4, 8, 128)
-    exchange("team", 4, lambda q: send4.at[q], lambda q: recv4.at[pl.ds(rows * q, rows)])
-    arrived(4, recv4)
-    exchange("gx", 5, lambda q: recv4.at[pl.ds(2 * q, 2)], lambda q: recv5.at[pl.ds(2 * q, 2)])
-    arrived(5, recv5)
+    for d in (2, 1, 3, 0):
+        m = lax.rem(member + d, 4)
+        for a in range(per):
+            q = per * member + a
+            straight(4, send4.at[m, 2 * a : 2 * a + 2], recv5.at[pl.ds(2 * ix, 2)], q, m, q == ix if d == 0 else None)
+    arrived(4, recv5)
     lines = []
     for y in range(8):
         got = recv5[:, y, :]
@@ -532,17 +563,21 @@
         one = wave[:kx, at] + rot(wave[kx:, at])
         for k in range(2):
             send8[pl.ds(8 * k + y, gx, stride=16), :] = one[k * gx : (k + 1) * gx]
-    exchange("gx", 8, lambda q: send8.at[pl.ds(pl.multiple_of(16 * q, 16), 16)], lambda q: recv8.at[pl.ds(pl.multiple_of(16 * q, 16), 16)])
+    block = 8 * rows
+    for k in range(gx):
+        at = 1 + (k + 3) % (gx - 1) if k < gx - 1 else 0
+        q = outward[at]
+        straight(
+            9,
+            send8.at[pl.ds(pl.multiple_of(16 * q, 16), 16)],
+            recv9.at[pl.ds(pl.multiple_of(block * member + 16 * lax.rem(ix, per), 16), 16)],
+            q,
+            holder,
+            same if at == 0 else None,
+        )
     arrived(12, recv12)
     send11[...] = recv12[...].reshape(gx, 128).sum(0, keepdims=True).reshape(1, 1, 128)
     exchange("gy", 11, lambda q: send11, lambda q: recv11.at[pl.ds(q, 1)])
-    arrived(8, recv8)
-    block = 8 * rows
-    exchange(
-        "team", 9,
-        lambda q: recv8.at[pl.ds(pl.multiple_of(block * q, block), block)],
-        lambda q: recv9.at[pl.ds(pl.multiple_of(block * q, block), block)],
-    )
     arrived(9, recv9)
     lines = []
     for r in range(rows):
@@ -573,17 +608,20 @@
         (1, recv1.at[1:gx]),
         (2, send2.at[2 : 2 * gy]),
         (3, recv3.at[rows : gy * rows]),
-        (4, recv4.at[rows:gy]),
-        (5, recv4.at[2 : 2 * gx]),
+        (4, recv5.at[2 : 2 * gx]),
         (6, send6.at[1:gx]),
         (7, send7.at[1:gx]),
-        (8, send8.at[16 : 16 * gx]),
-        (9, recv9.at[block : 4 * block]),
+        (9, send8.at[16 : 16 * gx]),
         (10, send10.at[rows : gy * rows]),
         (11, recv11.at[1:gy]),
         (12, recv12.at[1:gx]),
     ):
         pltpu.make_async_copy(whole, whole, send_sem.at[phase_id]).wait()
+
+    @pl.when(jnp.logical_not(same))
+    def _():
+        for phase_id, whole in ((4, recv5.at[0:2]), (9, send8.at[0:16])):
+            pltpu.make_async_copy(whole, whole, send_sem.at[phase_id]).wait()
 
 
 def finish(
@@ -666,8 +704,8 @@
         buf(4, 64, 128), buf(64, 2 * depth), buf(64, depth), buf(64, depth),
         buf(4 * width, 8, 128), buf(2, square), buf(4, gy, 128), buf(64 * group, 2 * depth), buf(128, 1, 128),
         buf(16 * gx, 128), buf(gx, 16, 128), buf(2 * gy, 1, 128), buf(2 * gy, 1, 128), buf(4, rows, 128), buf(gy * rows, 128),
-        buf(4, rows, 8, 128), buf(gy, 8, 128), buf(2 * gx, 8, 128), buf(gx, 8, 8, 128), buf(gx, 8, 8, 128),
-        buf(gx, 8, 8, 128), buf(gx, 8, 8, 128), buf(16 * gx, 128), buf(16 * gx, 128), buf(32 * rows, 128),
+        buf(4, rows, 8, 128), buf(2 * gx, 8, 128), buf(gx, 8, 8, 128), buf(gx, 8, 8, 128),
+        buf(gx, 8, 8, 128), buf(gx, 8, 8, 128), buf(16 * gx, 128), buf(32 * rows, 128),
         buf(gy * rows, 128), buf(gy * rows, 128), buf(1, 1, 128), buf(gy, 1, 128), buf(1, 1, 128), buf(gx, 1, 128),
         pltpu.SemaphoreType.DMA((12,)), pltpu.SemaphoreType.DMA((12,)),
         pltpu.SemaphoreType.DMA((13,)), pltpu.SemaphoreType.DMA((13,)), pltpu.SemaphoreType.DMA((gx,)),

time: 97.4 us -> 92.6 us (0.951)
  Pallas kernels: 95.9 us -> 91.8 us
    pallas_call x1, Pallas kernels: 93.7 us -> 89.6 us  [per_device(): pl.pallas_call(body, out_shape=outs, in_specs=[far_spec] * count, out_spe...]
where the time goes in v6:
time: 92.6 us; the launch traced here: 92.4 us
  Pallas kernels  91.8 us (99%)
    pallas_call x1, Pallas kernels, per_device(): pl.pallas_call(body, out_shape=outs, in_specs=[far_spec] * count, out_spe...  89.6 us
    pallas_call x1, Pallas kernels, per_device(): pl.pallas_call(lambda *refs: finish(scale, *refs), out_shape=finals, in_s...  2.18 us

profile of v6, /device:TPU:1, one launch (start us, length us, event | category | flops | bytes accessed | tf_op | source)
XLA Modules:
  0.0 92.4 jit_solution(12236102846236955996)
XLA Ops:
  0.6 89.6 %layer.1 = (f32[8,8,256]{2,1,0:T(8,128)}, f32[8,8,256]{2,1,0:T(8,128)}, f32[8,8,256]{2,1,0:T(8,128)}, f32[32,128]{1,0:T(8,128)}, f32[2,128]{1,0:T(2,128)}, /*index=5*/f32[1,128]{1,0:T(1,128)}) custom-call(f32[8,8,256]{2,1,0:T(8,128)} %refs_0_.1, f32[8,8,256]{2,1,0:T(8,128)} %refs_1_.1, f32[8,8,256]{2,1,0:T(8,128)} %refs_2_.1, f32[8,8,256]{2,1,0:T(8,128)} %refs_3_.1, ...), custom_call_target="tpu_custom_call" | custom-call | tf_op jit(solution)/shard_map/layer/pallas_call | solution.py:732
  90.2 2.2 %finish.1 = (f32[8,8,256]{2,1,0:T(8,128)}, f32[8,8,256]{2,1,0:T(8,128)}, f32[8,8,256]{2,1,0:T(8,128)}, f32[2,2,1,32,1024]{4,3,2,1,0:T(8,128)}, f32[32,32]{1,0:T(8,128)}, /*index=5*/f32[1,32]{1,0:T(1,128)}) custom-call(f32[8,8,256]{2,1,0:T(8,128)} %get-tuple-element.18.refs_0_, f32[8,8,256]{2,1,0:T(8,128)} %get-tuple-element.19.refs_1_, ...), custom_call_target="tpu_custom_call" | custom-call | tf_op jit(solution)/shard_map/finish/pallas_call | solution.py:743

commit v7 on v6

--- a/solution.py
+++ b/solution.py
@@ -173,7 +173,7 @@
     zf, zg, zi, tx, ty, tyi, txi, txf, tyf,
     phase_far, solute_far, predicted_far, modes_far, spec_far, added_far,
     phase_out, solute_out, predicted_out, spec_out, added_out, modes_out, out_sem,
-    yhi, ylo, from_ylo, from_yhi, from_corner, from_xlo, from_xhi,
+    yhi, ylo, thin, weave, from_ylo, from_yhi, from_corner, from_xlo, from_xhi,
     pad_p, pad_c, pad_d, pad_u, mid_p, mid_c, mid_d, flat, cells, cot, total, coef, lifted, blend, field, sums,
     send1, recv1, send2, recv2, send3, recv3, send4, recv5, send6, recv6, send7, recv7,
     send8, recv9, send10, recv10, send11, recv11, send12, recv12,
@@ -234,6 +234,11 @@
     p, c, u = phase[...], solute[...], undercool[...]
     yhi[...] = jnp.where(row >= 6, p, jnp.where(row >= 4, pltpu.roll(c, 6, 1), pltpu.roll(u, 4, 1)))
     ylo[...] = jnp.where(row < 2, p, jnp.where(row < 4, pltpu.roll(c, 2, 1), pltpu.roll(u, 4, 1)))
+    for k, (rows_ref, first) in enumerate(((yhi, 3), (ylo, 0))):
+        for h in range(2):
+            weave[h] = rows_ref[:, :, 128 * h : 128 * h + 128].reshape(64, 128)
+            for r in range(5):
+                thin[k, r, :, 128 * h : 128 * h + 128] = weave[h, pl.ds(first + r, 8, stride=8), :]
     pad_p[2:10, 8:16, :] = p
     pad_c[2:10, 8:16, :] = c
     pad_u[1:9, 8:16, :] = u
@@ -300,8 +305,8 @@
         return copy
 
     copies = [
-        push(yhi, from_ylo, 0, {"gy": north}),
-        push(ylo, from_yhi, 1, {"gy": south}),
+        push(thin.at[0], from_ylo, 0, {"gy": north}),
+        push(thin.at[1], from_yhi, 1, {"gy": south}),
         push(yhi.at[7], from_corner.at[0], 2, {"gx": east, "gy": north}),
         push(yhi.at[0], from_corner.at[1], 3, {"gx": west, "gy": north}),
         push(ylo.at[7], from_corner.at[2], 4, {"gx": east, "gy": south}),
@@ -323,8 +328,16 @@
         pad_c[planes, at, :] = pltpu.roll(rows, (2 * turn) % 8, 1)
         pad_u[slice(planes.start - 1, planes.stop - 1), at, :] = pltpu.roll(rows, 4, 1)
 
-    lay(from_ylo[...], True, slice(2, 10))
-    lay(from_yhi[...], False, slice(2, 10))
+    def planes_of(got, first):
+        halves = []
+        for h in range(2):
+            for r in range(5):
+                weave[h, pl.ds(first + r, 8, stride=8), :] = got[r, :, 128 * h : 128 * h + 128]
+            halves.append(weave[h].reshape(8, 8, 128))
+        return jnp.concatenate(halves, axis=2)
+
+    lay(planes_of(from_ylo, 3), True, slice(2, 10))
+    lay(planes_of(from_yhi, 0), False, slice(2, 10))
     lay(from_corner[0:1], True, slice(1, 2))
     lay(from_corner[1:2], True, slice(10, 11))
     lay(from_corner[2:3], False, slice(1, 2))
@@ -698,7 +711,7 @@
     outs = (tile, tile, tile, shape(gy, 128), shape(2, 128), shape(1, 128))
     scratch = [
         buf(8, 8, depth), buf(8, 8, depth), buf(8, 8, depth), buf(2, 128), buf(1, 128), buf(gy, 128), pltpu.SemaphoreType.DMA((6,)),
-        buf(8, 8, depth), buf(8, 8, depth), buf(8, 8, depth), buf(8, 8, depth), buf(4, 8, depth), buf(5, 8, depth), buf(5, 8, depth),
+        buf(8, 8, depth), buf(8, 8, depth), buf(2, 5, 8, depth), buf(2, 64, 128), buf(5, 8, depth), buf(5, 8, depth), buf(4, 8, depth), buf(5, 8, depth), buf(5, 8, depth),
         buf(12, 24, depth), buf(12, 24, depth), buf(12, 24, depth), buf(10, 24, depth),
         buf(10, 24, depth), buf(10, 24, depth), buf(10, 24, depth),
         buf(4, 64, 128), buf(64, 2 * depth), buf(64, depth), buf(64, depth),

time: 92.6 us -> 92.3 us (level)
  no operation moved by 1% of the time
where the time goes in v7:
time: 92.3 us; the launch traced here: 92.1 us
  Pallas kernels  91.4 us (99%)
    pallas_call x1, Pallas kernels, per_device(): pl.pallas_call(body, out_shape=outs, in_specs=[far_spec] * count, out_spe...  89.3 us
    pallas_call x1, Pallas kernels, per_device(): pl.pallas_call(lambda *refs: finish(scale, *refs), out_shape=finals, in_s...  2.18 us

profile of v7, /device:TPU:1, one launch (start us, length us, event | category | flops | bytes accessed | tf_op | source)
XLA Modules:
  0.0 92.1 jit_solution(14324037755794922657)
XLA Ops:
  0.6 89.3 %layer.1 = (f32[8,8,256]{2,1,0:T(8,128)}, f32[8,8,256]{2,1,0:T(8,128)}, f32[8,8,256]{2,1,0:T(8,128)}, f32[32,128]{1,0:T(8,128)}, f32[2,128]{1,0:T(2,128)}, /*index=5*/f32[1,128]{1,0:T(1,128)}) custom-call(f32[8,8,256]{2,1,0:T(8,128)} %refs_0_.1, f32[8,8,256]{2,1,0:T(8,128)} %refs_1_.1, f32[8,8,256]{2,1,0:T(8,128)} %refs_2_.1, f32[8,8,256]{2,1,0:T(8,128)} %refs_3_.1, ...), custom_call_target="tpu_custom_call" | custom-call | tf_op jit(solution)/shard_map/layer/pallas_call | solution.py:745
  89.9 2.2 %finish.1 = (f32[8,8,256]{2,1,0:T(8,128)}, f32[8,8,256]{2,1,0:T(8,128)}, f32[8,8,256]{2,1,0:T(8,128)}, f32[2,2,1,32,1024]{4,3,2,1,0:T(8,128)}, f32[32,32]{1,0:T(8,128)}, /*index=5*/f32[1,32]{1,0:T(1,128)}) custom-call(f32[8,8,256]{2,1,0:T(8,128)} %get-tuple-element.18.refs_0_, f32[8,8,256]{2,1,0:T(8,128)} %get-tuple-element.19.refs_1_, ...), custom_call_target="tpu_custom_call" | custom-call | tf_op jit(solution)/shard_map/finish/pallas_call | solution.py:756

commit v8 on v7

--- a/solution.py
+++ b/solution.py
@@ -140,10 +140,10 @@
     rate = total - 6.0 * p + p - p * p * p + COUPLING * squares * squares * (undercool - c)
     div = 0.0
     for dn, cn in zip(d_nb, c_nb):
-        div = div + 0.5 * (d + dn) * (cn - c)
+        div = div + (d + dn) * (cn - c)
     speed = TRAP_RATE * jnp.abs(rate)
     keff = (PARTITION + speed) / (1.0 + speed)
-    return p + TIME_STEP * rate, c + TIME_STEP * (div + 0.5 * (1.0 - keff) * c * rate)
+    return p + TIME_STEP * rate, c + TIME_STEP * 0.5 * (div + (1.0 - keff) * c * rate)
 
 
 def partners(ix, gx, sign):
@@ -371,7 +371,7 @@
             flat[2 + h, pl.ds(at, 8), :] = new_c[:, 128 * h : 128 * h + 128] - SOLUTE_MEAN
         return carry
 
-    lax.fori_loop(0, 12, first_diff, 0)
+    lax.fori_loop(0, 12, first_diff, 0, unroll=2)
     lax.fori_loop(0, 10, first, 0)
     lax.fori_loop(0, 8, second, 0)
     writes = [pltpu.make_async_copy(phase_out, phase_far, out_sem.at[0]), pltpu.make_async_copy(solute_out, solute_far, out_sem.at[1])]
@@ -528,7 +528,7 @@
                 return tuple(acc)
 
             zero = jnp.zeros((8, depth), F32)
-            acc = lax.fori_loop(0, 4, block, (zero,) * 6)
+            acc = lax.fori_loop(0, 4, block, (zero,) * 6, unroll=4)
             for par in range(2):
                 for k in range(3):
                     one = jnp.sum(acc[3 * par + k], axis=0, keepdims=True)

time: 92.3 us -> 92.4 us (level)
  no operation moved by 1% of the time
where the time goes in v8:
time: 92.4 us; the launch traced here: 92.2 us
  Pallas kernels  91.6 us (99%)
    pallas_call x1, Pallas kernels, per_device(): pl.pallas_call(body, out_shape=outs, in_specs=[far_spec] * count, out_spe...  89.4 us
    pallas_call x1, Pallas kernels, per_device(): pl.pallas_call(lambda *refs: finish(scale, *refs), out_shape=finals, in_s...  2.18 us

profile of v8, /device:TPU:1, one launch (start us, length us, event | category | flops | bytes accessed | tf_op | source)
XLA Modules:
  0.0 92.2 jit_solution(12095465120370855028)
XLA Ops:
  0.6 89.4 %layer.1 = (f32[8,8,256]{2,1,0:T(8,128)}, f32[8,8,256]{2,1,0:T(8,128)}, f32[8,8,256]{2,1,0:T(8,128)}, f32[32,128]{1,0:T(8,128)}, f32[2,128]{1,0:T(2,128)}, /*index=5*/f32[1,128]{1,0:T(1,128)}) custom-call(f32[8,8,256]{2,1,0:T(8,128)} %refs_0_.1, f32[8,8,256]{2,1,0:T(8,128)} %refs_1_.1, f32[8,8,256]{2,1,0:T(8,128)} %refs_2_.1, f32[8,8,256]{2,1,0:T(8,128)} %refs_3_.1, ...), custom_call_target="tpu_custom_call" | custom-call | tf_op jit(solution)/shard_map/layer/pallas_call | solution.py:745
  90.0 2.2 %finish.1 = (f32[8,8,256]{2,1,0:T(8,128)}, f32[8,8,256]{2,1,0:T(8,128)}, f32[8,8,256]{2,1,0:T(8,128)}, f32[2,2,1,32,1024]{4,3,2,1,0:T(8,128)}, f32[32,32]{1,0:T(8,128)}, /*index=5*/f32[1,32]{1,0:T(1,128)}) custom-call(f32[8,8,256]{2,1,0:T(8,128)} %get-tuple-element.18.refs_0_, f32[8,8,256]{2,1,0:T(8,128)} %get-tuple-element.19.refs_1_, ...), custom_call_target="tpu_custom_call" | custom-call | tf_op jit(solution)/shard_map/finish/pallas_call | solution.py:756
